TPU v7x, 32 devices: a whole 2x2x4 slice. The times are simulated.
32 devices in a mesh: fsdp: 32 (over z, y, x, core).
Axes of the slice: x: 2, y: 2, z: 4, core: 2. Of those that a mesh axis runs over, the one named last changes fastest.
Arguments:
- block_in: bfloat16 [8192, 768], P('fsdp'), may hold values from -6 to 6
- segment_ids: int32 [8192], P('fsdp'), may hold values from 0 to 8191, as said below
- live_count: int32 [32], P('fsdp'), may hold values from 128 to 256, as said below
- norm_gain: bfloat16 [768], P('fsdp'), may hold values from 0.099609375 to 1.8984375
- in_weight: bfloat16 [768, 3352], P('fsdp'), may hold values from -0.21875 to 0.21875
- conv_weight: bfloat16 [1792, 4], P('fsdp'), may hold values from -3 to 3
- conv_bias: bfloat16 [1792], P('fsdp'), may hold values from -3 to 3
- step_bias: float32 [24], replicated, may hold values from -6 to -3
- decay_log: float32 [24], replicated, may hold values from 0 to 2.5
- skip_gain: float32 [24], replicated, may hold values from 0.5 to 1.5
- gated_gain: bfloat16 [1536], P('fsdp'), may hold values from 0.099609375 to 1.8984375
- out_weight: bfloat16 [1536, 768], P('fsdp'), may hold values from -0.15625 to 0.15625
- out_cotangent: bfloat16 [8192, 768], P('fsdp'), may hold values from -6 to 6
Outputs:
- block_out: bfloat16 [8192, 768], P('fsdp')
- input_grad: float32 [8192, 768], P('fsdp')
- norm_gain_grad: float32 [768], P('fsdp')
- in_weight_grad: float32 [768, 3352], P('fsdp')
- conv_weight_grad: float32 [1792, 4], P('fsdp')
- conv_bias_grad: float32 [1792], P('fsdp')
- step_bias_grad: float32 [24], replicated
- decay_log_grad: float32 [24], replicated
- skip_gain_grad: float32 [24], replicated
- gated_gain_grad: float32 [1536], P('fsdp')
- out_weight_grad: float32 [1536, 768], P('fsdp')
Inputs may be any that keep to these rules, and one draw needn't show every extreme that they name: `segment_ids`: segment numbers never fall inside a device's 256 slots and no segment spans two devices; a segment holds 1 to 256 slots and one holds exactly 256; a device's first padding slot starts a new segment. `live_count`: live slots come first in each device's 256 slots; one device is full in every draw.
All inputs are finite; a program needn't handle non-finite values.
Results may differ from a plain program's by a relative error of at most 0.0098.
Values may be sent and summed in bfloat16 or wider, within the bound.
A program may use at most 128 MiB of HBM per device.

v0:
```python
from functools import partial

import jax
import jax.numpy as jnp
from jax import lax
from jax.sharding import PartitionSpec as P

DI = 1536
STATE = 128
HDIM = 64
KCONV = 4
SCAN_BLOCK = 128
HEADS = 24
CONV = 1792


EPSILON = 1e-05
HIGHEST = lax.Precision.HIGHEST


def rms_scale(values, gain_vec):
    return (
        values * lax.rsqrt(jnp.mean(values * values, axis=-1, keepdims=True) + EPSILON) * gain_vec
    )


def convolve(inputs, kernel_w, kernel_bias, segments):
    length = inputs.shape[0]
    conv_total = kernel_bias[None, :] + kernel_w[:, KCONV - 1][None, :] * inputs
    for offset in range(1, KCONV):
        moved_in = jnp.concatenate(
            [jnp.zeros((offset, inputs.shape[1]), inputs.dtype), inputs[: length - offset]], axis=0
        )
        earlier = jnp.concatenate(
            [jnp.full((offset,), -1, jnp.int32), segments[: length - offset]], axis=0
        )
        same_seg = (earlier == segments).astype(inputs.dtype)
        conv_total = (
            conv_total + kernel_w[:, KCONV - 1 - offset][None, :] * moved_in * same_seg[:, None]
        )
    return conv_total


def block_step(carry_state, pieces):
    values, keys_in, queries, step_sizes, logdecay, group_segs, before = pieces
    positions = jnp.arange(SCAN_BLOCK)
    lower_mask = positions[:, None] >= positions[None, :]
    running = jnp.dot(lower_mask.astype(logdecay.dtype), logdecay, precision=HIGHEST)
    same_seg = lower_mask & (group_segs[:, None] == group_segs[None, :])
    spread = running.T[:, :, None] - running.T[:, None, :]
    decay_mat = jnp.where(same_seg[None], jnp.exp(jnp.where(same_seg[None], spread, 0.0)), 0.0)
    intersection = jnp.dot(queries, keys_in.T, precision=HIGHEST)
    weights_all = decay_mat * intersection[None] * step_sizes.T[:, None, :]
    intra_out = jnp.einsum("hts,shp->thp", weights_all, values, precision=HIGHEST)
    carried = (group_segs == before).astype(logdecay.dtype)
    factor = carried[:, None] * jnp.exp(running)
    inter_out = (
        jnp.einsum("tn,hpn->thp", queries, carry_state, precision=HIGHEST) * factor[:, :, None]
    )
    tail_mask = (group_segs == group_segs[-1]).astype(logdecay.dtype)
    towards = jnp.exp(running[-1][None, :] - running) * tail_mask[:, None] * step_sizes
    fresh_state = jnp.einsum(
        "shp,sn->hpn", towards[:, :, None] * values, keys_in, precision=HIGHEST
    )
    new_state = fresh_state + (carried[-1] * jnp.exp(running[-1]))[:, None, None] * carry_state
    return (new_state, intra_out + inter_out)


def run_mixer(segments, projected, params):
    kernel_w, kernel_bias, bias_step, log_rate, skip_vec, gain_gated = params
    length = projected.shape[0]
    gating = projected[:, :DI]
    conv_in = projected[:, DI : DI + CONV]
    raw_step = projected[:, DI + CONV :]
    activated = jax.nn.silu(convolve(conv_in, kernel_w, kernel_bias, segments))
    values = activated[:, :DI].reshape(length, HEADS, HDIM)
    keys_in = activated[:, DI : DI + STATE]
    queries = activated[:, DI + STATE :]
    step_sizes = jax.nn.softplus(raw_step + bias_step[None, :])
    logdecay = -step_sizes * jnp.exp(log_rate)[None, :]
    block_count = length // SCAN_BLOCK
    group_segs = segments.reshape(block_count, SCAN_BLOCK)
    before = jnp.concatenate([jnp.full((1,), -1, jnp.int32), group_segs[:-1, -1]])
    pieces = (
        values.reshape(block_count, SCAN_BLOCK, HEADS, HDIM),
        keys_in.reshape(block_count, SCAN_BLOCK, STATE),
        queries.reshape(block_count, SCAN_BLOCK, STATE),
        step_sizes.reshape(block_count, SCAN_BLOCK, HEADS),
        logdecay.reshape(block_count, SCAN_BLOCK, HEADS),
        group_segs,
        before,
    )
    initial_state = jnp.zeros((HEADS, HDIM, STATE), projected.dtype)
    _, outputs = lax.scan(jax.checkpoint(block_step), initial_state, pieces)
    scanned = outputs.reshape(length, HEADS, HDIM) + skip_vec[None, :, None] * values
    gated = scanned.reshape(length, DI) * jax.nn.silu(gating)
    return rms_scale(gated, gain_gated)


def per_device(
    block_in,
    segment_ids,
    live_count,
    norm_gain,
    in_weight,
    conv_weight,
    conv_bias,
    step_bias,
    decay_log,
    skip_gain,
    gated_gain,
    out_weight,
    out_cotangent,
):
    in_full, out_full, gain_full, gated_full, kernel_full, kbias_full = (
        lax.all_gather(in_weight, "fsdp", axis=0, tiled=True),
        lax.all_gather(out_weight, "fsdp", axis=0, tiled=True),
        lax.all_gather(norm_gain, "fsdp", axis=0, tiled=True),
        lax.all_gather(gated_gain, "fsdp", axis=0, tiled=True),
        lax.all_gather(conv_weight, "fsdp", axis=0, tiled=True),
        lax.all_gather(conv_bias, "fsdp", axis=0, tiled=True),
    )
    row_count = block_in.shape[0]
    in_shape = in_weight.shape
    out_shape = out_weight.shape
    kernel_shape = conv_weight.shape
    gain_norm = gain_full.astype(jnp.float32)
    params = (
        kernel_full.astype(jnp.float32),
        kbias_full.astype(jnp.float32),
        step_bias,
        decay_log,
        skip_gain,
        gated_full.astype(jnp.float32),
    )
    source = block_in.astype(jnp.float32)
    live_rows = (lax.iota(jnp.int32, row_count) < live_count[0]).astype(jnp.float32)
    normed = rms_scale(source, gain_norm).astype(jnp.bfloat16)
    projected = jnp.dot(normed, in_full, preferred_element_type=jnp.float32)
    mixer_out, mixer_vjp = jax.vjp(partial(run_mixer, segment_ids), projected, params)
    mixer_low = mixer_out.astype(jnp.bfloat16)
    branch = jnp.dot(mixer_low, out_full, preferred_element_type=jnp.float32)
    output = (source + live_rows[:, None] * branch).astype(jnp.bfloat16)
    in_back, out_back = (
        lax.all_gather(in_weight, "fsdp", axis=0, tiled=True),
        lax.all_gather(out_weight, "fsdp", axis=0, tiled=True),
    )
    masked = jnp.where(live_rows[:, None] > 0, out_cotangent, jnp.zeros_like(out_cotangent))
    grad_out_w = lax.dot_general(
        mixer_low, masked, (((0,), (0,)), ((), ())), preferred_element_type=jnp.float32
    )
    grad_mixer = lax.dot_general(
        masked, out_back, (((1,), (1,)), ((), ())), preferred_element_type=jnp.float32
    )
    grad_proj, grad_params = mixer_vjp(grad_mixer)
    grad_low = grad_proj.astype(jnp.bfloat16)
    grad_in_w = lax.dot_general(
        normed, grad_low, (((0,), (0,)), ((), ())), preferred_element_type=jnp.float32
    )
    grad_normed = lax.dot_general(
        grad_low, in_back, (((1,), (1,)), ((), ())), preferred_element_type=jnp.float32
    )
    _, norm_vjp = jax.vjp(rms_scale, source, gain_norm)
    grad_source, grad_gain = norm_vjp(grad_normed)
    grad_input = out_cotangent.astype(jnp.float32) + grad_source
    shares = (
        lax.psum_scatter(grad_in_w.reshape(-1), "fsdp", scatter_dimension=0, tiled=True),
        lax.psum_scatter(grad_out_w.reshape(-1), "fsdp", scatter_dimension=0, tiled=True),
        lax.psum_scatter(grad_gain, "fsdp", scatter_dimension=0, tiled=True),
        lax.psum_scatter(grad_params[5], "fsdp", scatter_dimension=0, tiled=True),
        lax.psum_scatter(grad_params[0].reshape(-1), "fsdp", scatter_dimension=0, tiled=True),
        lax.psum_scatter(grad_params[1], "fsdp", scatter_dimension=0, tiled=True),
    )
    in_flat, out_flat, gain_share, gated_share, kernel_flat, kbias_share = shares
    in_share = in_flat.reshape(in_shape)
    out_share = out_flat.reshape(out_shape)
    kernel_share = kernel_flat.reshape(kernel_shape)
    summed = lax.psum((grad_params[2], grad_params[3], grad_params[4]), "fsdp")
    return (
        output,
        grad_input,
        gain_share,
        in_share,
        kernel_share,
        kbias_share,
        summed[0],
        summed[1],
        summed[2],
        gated_share,
        out_share,
    )


def solution(mesh):
    in_specs = (
        P("fsdp", None),
        P("fsdp"),
        P("fsdp"),
        P("fsdp"),
        P("fsdp", None),
        P("fsdp", None),
        P("fsdp"),
        P(),
        P(),
        P(),
        P("fsdp"),
        P("fsdp", None),
        P("fsdp", None),
    )
    out_specs = (
        P("fsdp", None),
        P("fsdp", None),
        P("fsdp"),
        P("fsdp", None),
        P("fsdp", None),
        P("fsdp"),
        P(),
        P(),
        P(),
        P("fsdp"),
        P("fsdp", None),
    )
    return jax.shard_map(
        per_device, mesh=mesh, in_specs=in_specs, out_specs=out_specs, check_vma=False
    )
```

profile of v0, /device:TPU:0, one launch (start us, length us, event | category | flops | bytes accessed | tf_op | source)
XLA Modules:
  0.0 632.1 jit_solution(4533442815971775762)
XLA Ops:
  15.6 42.4 %all-reduce.31 = (bf16[768]{0:T(1024)(128)(2,1)S(1)}, bf16[1792]{0:T(1024)(128)(2,1)S(1)}, bf16[1536]{0:T(1024)(128)(2,1)S(1)}) all-reduce(bf16[768]{0:T(1024)(128)(2,1)S(1)} %dynamic-update-slice, bf16[1792]{0:T(1024)(128)(2,1)S(1)} %dynamic-update-slice.1, bf16[1536]{0:T(1024)(128)(2,1)S(1)} %dynamic-update-slice.2), channel_id=1, replica_groups=mesh['fsdp'=32] {'fsdp'}, use_global_device_ids=true, to_apply=%add.20 | all-reduce | flops 4096 | bytes 16384
  59.4 40.8 %all-gather = bf16[32,56,4]{1,2,0:T(4,128)(2,1)S(1)} all-gather(bf16[1,56,4]{1,2,0:T(4,128)(2,1)} %bitcast.348), channel_id=1, replica_groups=mesh['fsdp'=32] {'fsdp'}, dimensions={0}, use_global_device_ids=true | all-gather | bytes 14784 | tf_op jit(solution)/shard_map/all_gather | solution.py:120
  102.2 4.9 fusion.126
  110.0 4.0 fusion.108
  122.5 63.4 %while.42 = (s32[]{:T(128)}, f32[24,64,128]{2,1,0:T(8,128)S(1)}, f32[2,128,24,64]{1,0,3,2:T(2,128)}, f32[2,24,64,128]{3,2,1,0:T(8,128)}, f32[2,128,24]{1,2,0:T(8...) while((s32[]{:T(128)}, f32[24,64,128]{2,1,0:T(8,128)S(1)}, ...), condition=%wide.region_2.3_spmd.clone, body=%wide.region_1.2_spmd.clone.sunk | while | flops 939487744 | bytes 10031308 | solution.py:94
  129.0 3.3 fusion.222
  133.0 19.0 %dynamic_update_slice.79 = f32[2,128,24,64]{1,0,3,2:T(2,128)} dynamic-update-slice(f32[2,128,24,64]{1,0,3,2:T(2,128)} %get-tuple-element.1142, f32[1,128,24,64]{1,0,3,2:T(1,128)S(1)} %bitcast.323, s32[]{:T(128)S(6)} %copy.230, s32[]{:T(128)} %constant.118.clone.1..sunk, s32[]{:T(128)} %constant.118.clone.1..sunk, s32[]{:T(128)} %constant.118.clone.1..sunk) | dynamic-update-slice | bytes 1572868 | tf_op jit(solution)/shard_map/jvp()/while/body/jit(dynamic_update_index_in_dim)/dynamic_update_slice | solution.py:94
  164.8 19.0 %dynamic_update_slice.79 = f32[2,128,24,64]{1,0,3,2:T(2,128)} dynamic-update-slice(f32[2,128,24,64]{1,0,3,2:T(2,128)} %get-tuple-element.1142, f32[1,128,24,64]{1,0,3,2:T(1,128)S(1)} %bitcast.323, s32[]{:T(128)S(6)} %copy.230, s32[]{:T(128)} %constant.118.clone.1..sunk, s32[]{:T(128)} %constant.118.clone.1..sunk, s32[]{:T(128)} %constant.118.clone.1..sunk) | dynamic-update-slice | bytes 1572868 | tf_op jit(solution)/shard_map/jvp()/while/body/jit(dynamic_update_index_in_dim)/dynamic_update_slice | solution.py:94
  192.0 3.6 multiply_reduce_fusion.8
  195.6 4.7 multiply_reduce_fusion.9
  207.7 111.8 %while.43 = (s32[]{:T(128)}, f32[24,64,128]{2,1,0:T(8,128)}, f32[2,128,24,64]{1,0,3,2:T(2,128)}, f32[2,128,128]{2,1,0:T(8,128)}, f32[2,128,128]{2,1,0:T(8,128)},...) while((s32[]{:T(128)}, f32[24,64,128]{2,1,0:T(8,128)}, ...), condition=%wide.region_14.15_spmd.clone, body=%wide.region_5.14_spmd.clone.sunk | while | flops 2209634816 | bytes 52391952 | solution.py:94
  224.3 4.4 fusion.247
  243.9 19.0 %dynamic_update_slice.82 = f32[2,128,24,64]{1,0,3,2:T(2,128)} dynamic-update-slice(f32[2,128,24,64]{1,0,3,2:T(2,128)} %get-tuple-element.1186, f32[1,128,24,64]{1,0,3,2:T(1,128)} %bitcast.324, s32[]{:T(128)S(6)} %sub.252, s32[]{:T(128)} %constant.118.clone.1..sunk.1, s32[]{:T(128)} %constant.118.clone.1..sunk.1, s32[]{:T(128)} %constant.118.clone.1..sunk.1) | dynamic-update-slice | bytes 1572868 | tf_op jit(solution)/shard_map/transpose(jvp())/while/body/jit(dynamic_update_index_in_dim)/dynamic_update_slice | solution.py:94
  280.4 4.4 fusion.247
  300.0 19.0 %dynamic_update_slice.82 = f32[2,128,24,64]{1,0,3,2:T(2,128)} dynamic-update-slice(f32[2,128,24,64]{1,0,3,2:T(2,128)} %get-tuple-element.1186, f32[1,128,24,64]{1,0,3,2:T(1,128)} %bitcast.324, s32[]{:T(128)S(6)} %sub.252, s32[]{:T(128)} %constant.118.clone.1..sunk.1, s32[]{:T(128)} %constant.118.clone.1..sunk.1, s32[]{:T(128)} %constant.118.clone.1..sunk.1) | dynamic-update-slice | bytes 1572868 | tf_op jit(solution)/shard_map/transpose(jvp())/while/body/jit(dynamic_update_index_in_dim)/dynamic_update_slice | solution.py:94
  324.5 3.4 multiply_reduce_fusion.7
  336.0 6.1 reshape.369
  342.9 4.0 fusion.140
  348.1 5.8 fusion.124
  353.9 11.7 %reshape.365 = f32[2574336]{0:T(1024)} reshape(f32[768,3352]{1,0:T(8,128)} %fusion.124) | data formatting | bytes 20594688 | tf_op jit(solution)/shard_map/reshape | solution.py:167
  367.6 5.1 fusion.116
  372.7 39.8 %all-reduce.29 = (f32[768]{0:T(1024)S(1)}, f32[7168]{0:T(1024)S(1)}, f32[1792]{0:T(1024)S(1)}, f32[24]{0:T(128)}, f32[24]{0:T(128)}, /*index=5*/f32[24]{0:T(128)}, f32[1536]{0:T(1024)S(1)}) all-reduce(f32[768]{0:T(1024)S(1)} %get-tuple-element.778, f32[7168]{0:T(1024)S(1)} %reshape.367, ...), channel_id=2, replica_groups=mesh['fsdp'=32] {'fsdp'}, use_global_device_ids=true, to_apply=%region_17.18.clone | all-reduce | flops 11336 | bytes 90688
  416.3 3.4 fusion.112
  419.7 202.0 %all-reduce.34.cloned.1.call-done = (f32[2574336]{0:T(1024)}, f32[1179648]{0:T(1024)}) async-done(((f32[2574336]{0:T(1024)}, f32[1179648]{0:T(1024)}), (f32[2574336]{0:T(1024)}, f32[1179648]{0:T(1024)})) %all-reduce.34.cloned.1.call-update) | async-done | bytes 15015952
  (382 shorter events, 145.7 us)
Async XLA Ops:
  7.2 95.0 %all-gather.4.cloned.1.call-start = ((), (), s32[]{:S(2)}) async-start(), calls=%async_computation | async-start | bytes 5474304 | tf_op jit(solution)/shard_map/all_gather | solution.py:116
  7.9 184.1 %all-gather.6.cloned.1.call-start = ((), (), s32[]{:S(2)}) async-start(), calls=%async_computation.1 | async-start | bytes 2433024 | tf_op jit(solution)/shard_map/all_gather | solution.py:117
  8.7 613.0 %all-reduce.34.cloned.1.call-start = ((), (), s32[]{:S(2)}) async-start(), calls=%async_computation.2 | async-start | bytes 30031872
  11.3 107.8 %copy-start.69 = (f32[24]{0:T(128)}, f32[24]{0:T(128)S(1)}, u32[]{:S(2)}) copy-start(f32[24]{0:T(128)S(1)} %exp.97) | copy-start | bytes 292
  13.0 94.1 %copy-start.56 = (f32[256]{0:T(256)}, f32[256]{0:T(256)S(1)}, u32[]{:S(2)}) copy-start(f32[256]{0:T(256)S(1)} %fusion.134) | copy-start | bytes 3076
  58.0 137.6 %copy-start.33 = (f32[1536]{0:T(1024)}, f32[1536]{0:T(1024)S(1)}, u32[]{:S(2)}) copy-start(f32[1536]{0:T(1024)S(1)} %convert_element_type.103) | copy-start | bytes 18436
  100.5 7.1 %copy-start.43 = (f32[1792]{0:T(1024)}, f32[1792]{0:T(1024)S(1)}, u32[]{:S(2)}) copy-start(f32[1792]{0:T(1024)S(1)} %get-tuple-element.780) | copy-start | bytes 21508
  100.5 7.1 %copy-start.45 = (f32[1792]{0:T(1024)}, f32[1792]{0:T(1024)S(1)}, u32[]{:S(2)}) copy-start(f32[1792]{0:T(1024)S(1)} %get-tuple-element.781) | copy-start | bytes 21508
  100.5 7.1 %copy-start.47 = (f32[1792]{0:T(1024)}, f32[1792]{0:T(1024)S(1)}, u32[]{:S(2)}) copy-start(f32[1792]{0:T(1024)S(1)} %get-tuple-element.783) | copy-start | bytes 21508
  133.0 19.9 %copy-start.58 = (f32[24]{0:T(128)S(1)}, f32[24]{0:T(128)}, u32[]{:S(2)}) copy-start(f32[24]{0:T(128)} %exponential_multiply_fusion.10) | copy-start | bytes 292 | tf_op jit(solution)/shard_map/jvp()/while
  164.8 19.9 %copy-start.58 = (f32[24]{0:T(128)S(1)}, f32[24]{0:T(128)}, u32[]{:S(2)}) copy-start(f32[24]{0:T(128)} %exponential_multiply_fusion.10) | copy-start | bytes 292 | tf_op jit(solution)/shard_map/jvp()/while
  221.2 8.3 %copy-start.36 = (f32[24]{0:T(128)}, f32[24]{0:T(128)S(1)}, u32[]{:S(2)}) copy-start(f32[24]{0:T(128)S(1)} %get-tuple-element.1110) | copy-start | bytes 292 | tf_op jit(solution)/shard_map/transpose(jvp())/while
  238.1 24.8 %copy-start.3 = (f32[2,128,24,64]{1,3,2,0:T(8,128)S(1)}, f32[2,128,24,64]{1,3,2,0:T(8,128)}, u32[]{:S(2)}) copy-start(f32[2,128,24,64]{1,3,2,0:T(8,128)} %copy-done.2) | copy-start | bytes 4718596 | tf_op jit(solution)/shard_map/transpose(jvp())/while
  238.1 24.8 %copy-start.28 = (f32[2,128,24]{1,2,0:T(8,128)S(1)}, f32[2,128,24]{1,2,0:T(8,128)}, u32[]{:S(2)}) copy-start(f32[2,128,24]{1,2,0:T(8,128)} %copy-done.27) | copy-start | bytes 73732 | tf_op jit(solution)/shard_map/transpose(jvp())/while
  238.1 24.8 %copy-start.78 = (s32[2]{0:T(128)S(1)}, s32[2]{0:T(128)}, u32[]{:S(2)}) copy-start(s32[2]{0:T(128)} %copy-done.77) | copy-start | bytes 28 | tf_op jit(solution)/shard_map/transpose(jvp())/while
  277.4 8.3 %copy-start.36 = (f32[24]{0:T(128)}, f32[24]{0:T(128)S(1)}, u32[]{:S(2)}) copy-start(f32[24]{0:T(128)S(1)} %get-tuple-element.1110) | copy-start | bytes 292 | tf_op jit(solution)/shard_map/transpose(jvp())/while
  294.3 24.8 %copy-start.3 = (f32[2,128,24,64]{1,3,2,0:T(8,128)S(1)}, f32[2,128,24,64]{1,3,2,0:T(8,128)}, u32[]{:S(2)}) copy-start(f32[2,128,24,64]{1,3,2,0:T(8,128)} %copy-done.2) | copy-start | bytes 4718596 | tf_op jit(solution)/shard_map/transpose(jvp())/while
  294.3 24.8 %copy-start.28 = (f32[2,128,24]{1,2,0:T(8,128)S(1)}, f32[2,128,24]{1,2,0:T(8,128)}, u32[]{:S(2)}) copy-start(f32[2,128,24]{1,2,0:T(8,128)} %copy-done.27) | copy-start | bytes 73732 | tf_op jit(solution)/shard_map/transpose(jvp())/while
  294.3 24.8 %copy-start.78 = (s32[2]{0:T(128)S(1)}, s32[2]{0:T(128)}, u32[]{:S(2)}) copy-start(s32[2]{0:T(128)} %copy-done.77) | copy-start | bytes 28 | tf_op jit(solution)/shard_map/transpose(jvp())/while
  367.5 47.6 %copy-start.66 = (f32[256]{0:T(256)S(1)}, f32[256]{0:T(256)}, u32[]{:S(2)}) copy-start(f32[256]{0:T(256)} %copy-done.65) | copy-start | bytes 3076
  367.5 47.6 %copy-start.24 = (bf16[256,768]{1,0:T(8,128)(2,1)S(1)}, bf16[256,768]{1,0:T(8,128)(2,1)}, u32[]{:S(2)}) copy-start(bf16[256,768]{1,0:T(8,128)(2,1)} %param.29) | copy-start | bytes 1179652
  372.7 43.6 %copy-start.5 = (f32[256,1536]{0,1:T(8,128)S(1)}, f32[256,1536]{0,1:T(8,128)}, u32[]{:S(2)}) copy-start(f32[256,1536]{0,1:T(8,128)} %copy-done.4) | copy-start | bytes 4718596
  372.7 43.6 %copy-start.34 = (f32[1536]{0:T(1024)S(1)}, f32[1536]{0:T(1024)}, u32[]{:S(2)}) copy-start(f32[1536]{0:T(1024)} %copy-done.33) | copy-start | bytes 18436
  372.7 43.6 %copy-start.52 = (f32[256]{0:T(256)S(1)}, f32[256]{0:T(256)}, u32[]{:S(2)}) copy-start(f32[256]{0:T(256)} %copy-done.51) | copy-start | bytes 3076
  (80 other events, 264.9 us)
Sparse Core Ops, SparseCore 0:
  10.9 68.5 all-gather.3
  82.4 55.4 all-gather.5
  365.8 255.8 all-reduce.33
where the time goes:
time: 643 us; the launch traced here: 632 us
  waiting for transfers between devices  203 us (32%)
  local copies, waits for them, and re-layouts  158 us (25%)
  blocking collectives  123 us (19%)
  matrix products  70.3 us (11%)
  other arithmetic  60.3 us (9%)
  between operations  15.5 us (2%)
    unnamed x4, waiting for transfers between devices  203 us
    unnamed x2, blocking collectives  82.2 us
    dynamic_update_slice x8, local copies, waits for them, and re-layouts, run_mixer(): _, outputs = lax.scan(jax.checkpoint(block_step), initial_state, pieces)  81.5 us
    all_gather x1, blocking collectives, per_device(): lax.all_gather(conv_weight, 'fsdp', axis=0, tiled=True)  40.8 us
    dot_general x6, matrix products, block_step(): jnp.einsum('hts,shp->thp', weights_all, values, precision=HIGHEST)  20.8 us
    unnamed x131, local copies, waits for them, and re-layouts  15 us
  transfers between devices with their start and end apart: 3, of which 1 were waited for; matrix products, arithmetic and copies ran while one was open for 17% of the time, Pallas kernels for 0%

commit v1 on v0

v1 whole, which is shorter than its diff:
```python
import functools

import jax
import jax.numpy as jnp
from jax import lax
from jax.experimental import pallas as pl
from jax.experimental.pallas import tpu as pltpu
from jax.sharding import PartitionSpec as P

DI = 1536
STATE = 128
HDIM = 64
KCONV = 4
HEADS = 24
CONV = 1792
LANES = 128
EPSILON = 1e-05
HIGHEST = lax.Precision.HIGHEST
F32 = jnp.float32
BF16 = jnp.bfloat16
NT = (((1,), (1,)), ((), ()))
TN = (((0,), (0,)), ((), ()))


def rms_scale(values, gain_vec):
    return (
        values * lax.rsqrt(jnp.mean(values * values, axis=-1, keepdims=True) + EPSILON) * gain_vec
    )


def dot(a, b, dims=(((1,), (0,)), ((), ()))):
    return lax.dot_general(a.astype(BF16), b.astype(BF16), dims, preferred_element_type=F32)


def sigmoid(v):
    return 1.0 / (1.0 + jnp.exp(-v))


def softplus(v):
    return jnp.maximum(v, 0.0) + jnp.log1p(jnp.exp(-jnp.abs(v)))


def chunk_ds(i):
    return pl.ds(pl.multiple_of(i * LANES, LANES), LANES)


def head_prelude(raw_ref, segc, segr, bias_ref, rate_ref):
    length = raw_ref.shape[0]
    rows = lax.broadcasted_iota(jnp.int32, (length, length), 0)
    cols = lax.broadcasted_iota(jnp.int32, (length, length), 1)
    mask = ((rows >= cols) & (segc == segr)).astype(F32)
    shifted = raw_ref[...] + bias_ref[...]
    step = softplus(shifted)
    decay = -step * rate_ref[...]
    running = jnp.dot(mask, decay, precision=HIGHEST, preferred_element_type=F32)
    return mask, shifted, step, decay, running


def column(values, h):
    lane = lax.broadcasted_iota(jnp.int32, values.shape, 1)
    return jnp.sum(jnp.where(lane == h, values, 0.0), axis=1, keepdims=True)


def decay_of(mask_ref, run_ref, run_t_ref, h):
    spread = column(run_ref[...], h) - run_t_ref[pl.ds(h, 1), :]
    mask = mask_ref[...]
    return jnp.where(mask > 0, jnp.exp(jnp.where(mask > 0, spread, 0.0)), 0.0)


def forward_kernel(
    proj_ref, raw_ref, segc_ref, segr_ref, shift_ref, cw_ref, bias_ref, rate_ref, skip_ref, gain_ref,
    pre_ref, scan_ref, low_ref,
    mask_s, run_s, runt_s, stept_s, inter_s, gated_s,
):
    length = proj_ref.shape[0]
    mask, _, step, _, running = head_prelude(
        raw_ref, segc_ref[...], segr_ref[...], bias_ref, rate_ref
    )
    mask_s[...] = mask
    run_s[...] = running
    runt_s[...] = running.T
    stept_s[...] = step.T

    def conv(i, _):
        ds = chunk_ds(i)
        x = proj_ref[:, chunk_ds(i + DI // LANES)]
        total = cw_ref[KCONV : KCONV + 1, ds] + cw_ref[KCONV - 1 : KCONV, ds] * x
        for j in range(1, KCONV):
            moved = pltpu.roll(x, j, 0) * shift_ref[:, j - 1 : j]
            total = total + cw_ref[KCONV - 1 - j : KCONV - j, ds] * moved
        pre_ref[:, ds] = total
        return 0

    lax.fori_loop(0, CONV // LANES, conv, 0)
    pre_k = pre_ref[:, DI : DI + STATE]
    pre_q = pre_ref[:, DI + STATE :]
    inter_s[...] = dot(pre_q * sigmoid(pre_q), pre_k * sigmoid(pre_k), NT)

    def pair(i, sumsq):
        ds = chunk_ds(i)
        pre = pre_ref[:, ds]
        values = pre * sigmoid(pre)
        low = values.astype(BF16)
        outs = []
        for side in range(2):
            h = 2 * i + side
            weights = decay_of(mask_s, run_s, runt_s, h) * inter_s[...] * stept_s[pl.ds(h, 1), :]
            outs.append(dot(weights, low))
        lane = lax.broadcasted_iota(jnp.int32, (length, LANES), 1)
        scanned = jnp.where(lane < HDIM, outs[0], outs[1]) + skip_ref[:, ds] * values
        scan_ref[:, ds] = scanned
        z = proj_ref[:, ds]
        gated = scanned * (z * sigmoid(z))
        gated_s[:, ds] = gated
        return sumsq + gated * gated

    sumsq = lax.fori_loop(0, DI // LANES, pair, jnp.zeros((length, LANES), F32))
    scale = lax.rsqrt(jnp.sum(sumsq, axis=1, keepdims=True) / DI + EPSILON)

    def finish(i, _):
        ds = chunk_ds(i)
        low_ref[:, ds] = (gated_s[:, ds] * scale * gain_ref[:, ds]).astype(BF16)
        return 0

    lax.fori_loop(0, DI // LANES, finish, 0)


def backward_kernel(
    proj_ref, raw_ref, segc_ref, segr_ref, shift_ref, cw_ref, bias_ref, rate_ref, skip_ref, gain_ref,
    pre_ref, scan_ref, gm_ref,
    glow_ref, graw_ref, gconv_ref, gdi_ref, ghead_ref,
    mask_s, run_s, runt_s, stept_s, inter_s, dinter_s, row_s, col_s,
):
    length = proj_ref.shape[0]
    mask, shifted, step, decay, running = head_prelude(
        raw_ref, segc_ref[...], segr_ref[...], bias_ref, rate_ref
    )
    mask_s[...] = mask
    run_s[...] = running
    runt_s[...] = running.T
    stept_s[...] = step.T
    pre_k = pre_ref[:, DI : DI + STATE]
    pre_q = pre_ref[:, DI + STATE :]
    keys = (pre_k * sigmoid(pre_k)).astype(BF16)
    queries = (pre_q * sigmoid(pre_q)).astype(BF16)
    inter_s[...] = dot(queries, keys, NT)
    dinter_s[...] = jnp.zeros_like(dinter_s)
    row_s[...] = jnp.zeros_like(row_s)
    col_s[...] = jnp.zeros_like(col_s)
    gconv_ref[...] = jnp.zeros_like(gconv_ref)
    gdi_ref[...] = jnp.zeros_like(gdi_ref)
    ghead_ref[...] = jnp.zeros_like(ghead_ref)

    def sums(i, carry):
        sumsq, inner = carry
        ds = chunk_ds(i)
        z = proj_ref[:, ds]
        gated = scan_ref[:, ds] * (z * sigmoid(z))
        return sumsq + gated * gated, inner + gated * gm_ref[:, ds] * gain_ref[:, ds]

    zero = jnp.zeros((length, LANES), F32)
    sumsq, inner = lax.fori_loop(0, DI // LANES, sums, (zero, zero))
    scale = lax.rsqrt(jnp.sum(sumsq, axis=1, keepdims=True) / DI + EPSILON)
    coef = scale * scale * scale * (jnp.sum(inner, axis=1, keepdims=True) / DI)

    def conv_back(i, grad_act):
        ds = chunk_ds(i)
        wide = chunk_ds(i + DI // LANES)
        pre = pre_ref[:, ds]
        sg = sigmoid(pre)
        gpre = grad_act * (sg * (1.0 + pre * (1.0 - sg)))
        x = proj_ref[:, wide]
        total = cw_ref[KCONV - 1 : KCONV, ds] * gpre
        gconv_ref[KCONV : KCONV + 1, ds] = jnp.sum(gpre, axis=0, keepdims=True)
        gconv_ref[KCONV - 1 : KCONV, ds] = jnp.sum(gpre * x, axis=0, keepdims=True)
        for j in range(1, KCONV):
            live = gpre * shift_ref[:, j - 1 : j]
            back = pltpu.roll(live, length - j, 0)
            total = total + cw_ref[KCONV - 1 - j : KCONV - j, ds] * back
            gconv_ref[KCONV - 1 - j : KCONV - j, ds] = jnp.sum(back * x, axis=0, keepdims=True)
        glow_ref[:, wide] = total.astype(BF16)

    def pair(i, _):
        ds = chunk_ds(i)
        z = proj_ref[:, ds]
        sz = sigmoid(z)
        silu_z = z * sz
        scanned = scan_ref[:, ds]
        gated = scanned * silu_z
        grad_out = gm_ref[:, ds]
        gdi_ref[0:1, ds] = jnp.sum(grad_out * gated * scale, axis=0, keepdims=True)
        dgated = scale * (grad_out * gain_ref[:, ds]) - gated * coef
        dscan = dgated * silu_z
        glow_ref[:, ds] = (dgated * scanned * (sz * (1.0 + z * (1.0 - sz)))).astype(BF16)
        pre = pre_ref[:, ds]
        values = pre * sigmoid(pre)
        gdi_ref[1:2, ds] = jnp.sum(dscan * values, axis=0, keepdims=True)
        low = values.astype(BF16)
        dlow = dscan.astype(BF16)
        lane = lax.broadcasted_iota(jnp.int32, (length, LANES), 1)
        head_lane = lax.broadcasted_iota(jnp.int32, (length, LANES), 1)
        outs = []
        for side in range(2):
            h = 2 * i + side
            here = (lane < HDIM) if side == 0 else (lane >= HDIM)
            factor = decay_of(mask_s, run_s, runt_s, h)
            stept = stept_s[pl.ds(h, 1), :]
            inter = inter_s[...]
            scaled = factor * stept
            outs.append(dot(scaled * inter, dlow, TN))
            dweights = dot(jnp.where(here, dscan, 0.0), low, NT)
            dinter_s[...] += dweights * scaled
            pairs = dweights * factor * inter
            col_s[pl.ds(h, 1), :] = jnp.sum(pairs, axis=0, keepdims=True)
            row = jnp.sum(pairs * stept, axis=1, keepdims=True)
            row_s[...] += jnp.where(head_lane == h, row, 0.0)
        grad_values = jnp.where(lane < HDIM, outs[0], outs[1]) + skip_ref[:, ds] * dscan
        conv_back(i, grad_values)
        return 0

    lax.fori_loop(0, DI // LANES, pair, 0)
    dinter = dinter_s[...].astype(BF16)
    conv_back(DI // LANES, dot(dinter, queries, TN))
    conv_back(DI // LANES + 1, dot(dinter, keys))
    dstep = col_s[...].T
    drun = row_s[...] - dstep * step
    ddecay = lax.dot_general(
        mask_s[...], drun, TN, precision=HIGHEST, preferred_element_type=F32
    )
    dstep = dstep - ddecay * rate_ref[...]
    graw = dstep * sigmoid(shifted)
    graw_ref[...] = graw.astype(BF16)
    ghead_ref[0:1, :] = jnp.sum(graw, axis=0, keepdims=True)
    ghead_ref[1:2, :] = jnp.sum(ddecay * decay, axis=0, keepdims=True)


def forward_mixer(proj, raw, small):
    length = proj.shape[0]
    vec = pltpu.VMEM
    return pl.pallas_call(
        forward_kernel,
        out_shape=(
            jax.ShapeDtypeStruct((length, CONV), F32),
            jax.ShapeDtypeStruct((length, DI), F32),
            jax.ShapeDtypeStruct((length, DI), BF16),
        ),
        in_specs=[pl.BlockSpec(memory_space=vec)] * 10,
        out_specs=[pl.BlockSpec(memory_space=vec)] * 3,
        scratch_shapes=[
            pltpu.VMEM((length, length), F32),
            pltpu.VMEM((length, LANES), F32),
            pltpu.VMEM((LANES, length), F32),
            pltpu.VMEM((LANES, length), F32),
            pltpu.VMEM((length, length), F32),
            pltpu.VMEM((length, DI), F32),
        ],
        compiler_params=pltpu.CompilerParams(vmem_limit_bytes=40 * 2**20),
        cost_estimate=pl.CostEstimate(
            flops=HEADS * length * length * 280, bytes_accessed=length * 30000, transcendentals=0
        ),
        name="mixer_forward",
    )(proj, raw, *small)


def backward_mixer(proj, raw, small, pre, scanned, grad_mixer):
    length, width = proj.shape[0], DI + CONV
    vec = pltpu.VMEM
    return pl.pallas_call(
        backward_kernel,
        out_shape=(
            jax.ShapeDtypeStruct((length, width), BF16),
            jax.ShapeDtypeStruct((length, LANES), BF16),
            jax.ShapeDtypeStruct((8, CONV), F32),
            jax.ShapeDtypeStruct((8, DI), F32),
            jax.ShapeDtypeStruct((8, LANES), F32),
        ),
        in_specs=[pl.BlockSpec(memory_space=vec)] * 13,
        out_specs=[pl.BlockSpec(memory_space=vec)] * 5,
        scratch_shapes=[
            pltpu.VMEM((length, length), F32),
            pltpu.VMEM((length, LANES), F32),
            pltpu.VMEM((LANES, length), F32),
            pltpu.VMEM((LANES, length), F32),
            pltpu.VMEM((length, length), F32),
            pltpu.VMEM((length, length), F32),
            pltpu.VMEM((length, LANES), F32),
            pltpu.VMEM((LANES, length), F32),
        ],
        compiler_params=pltpu.CompilerParams(vmem_limit_bytes=40 * 2**20),
        cost_estimate=pl.CostEstimate(
            flops=HEADS * length * length * 800, bytes_accessed=length * 60000, transcendentals=0
        ),
        name="mixer_backward",
    )(proj, raw, *small, pre, scanned, grad_mixer)


def per_device(
    block_in,
    segment_ids,
    live_count,
    norm_gain,
    in_weight,
    conv_weight,
    conv_bias,
    step_bias,
    decay_log,
    skip_gain,
    gated_gain,
    out_weight,
    out_cotangent,
):
    devices = lax.axis_size("fsdp")
    length = block_in.shape[0]
    share, proj_width = in_weight.shape
    width = block_in.shape[1]
    smalls = jnp.concatenate(
        [norm_gain, conv_weight.T.reshape(-1), conv_bias, gated_gain]
    )
    small_cols = -(-smalls.shape[0] // share)
    fold = out_weight.size // share
    used = proj_width + fold + small_cols
    padded = -(-used // LANES) * LANES
    packed = jnp.concatenate(
        [
            out_weight.reshape(share, fold),
            in_weight,
            jnp.pad(smalls, (0, share * (padded - proj_width - fold) - smalls.shape[0])).reshape(
                share, padded - proj_width - fold
            ),
        ],
        axis=1,
    )
    everything = lax.all_gather(packed, "fsdp", axis=0, tiled=True)
    in_full = everything[:, fold : fold + proj_width]
    out_full = everything[:, :fold].reshape(devices * out_weight.shape[0], width)
    rest = everything[:, fold + proj_width :].reshape(devices, -1).astype(F32)
    a = norm_gain.shape[0]
    b = a + conv_weight.size
    c = b + conv_bias.shape[0]
    d = c + gated_gain.shape[0]
    gain_norm = rest[:, :a].reshape(-1)
    kernel_rows = jnp.moveaxis(rest[:, a:b].reshape(devices, KCONV, -1), 1, 0).reshape(KCONV, CONV)
    kernel_bias = rest[:, b:c].reshape(1, CONV)
    gated = rest[:, c:d].reshape(1, DI)
    conv_rows = jnp.concatenate([kernel_rows, kernel_bias, jnp.zeros((3, CONV), F32)], axis=0)

    def lanes(v):
        return jnp.pad(v, (0, LANES - v.shape[0])).reshape(1, LANES)

    slots = jnp.arange(length)
    shift = jnp.stack(
        [
            ((slots >= j) & (jnp.roll(segment_ids, j) == segment_ids)).astype(F32)
            for j in range(1, KCONV)
        ],
        axis=1,
    )
    shift = jnp.pad(shift, ((0, 0), (0, 8 - shift.shape[1])))
    small = (
        segment_ids.reshape(length, 1),
        segment_ids.reshape(1, length),
        shift,
        conv_rows,
        lanes(step_bias),
        lanes(jnp.exp(decay_log)),
        jnp.repeat(skip_gain, HDIM).reshape(1, DI),
        gated,
    )
    source = block_in.astype(F32)
    live_rows = (lax.iota(jnp.int32, length) < live_count[0]).astype(F32)
    masked = jnp.where(live_rows[:, None] > 0, out_cotangent, jnp.zeros_like(out_cotangent))
    normed = rms_scale(source, gain_norm).astype(BF16)
    main = DI + CONV
    projected = jnp.dot(normed, in_full[:, :main], preferred_element_type=F32)
    tail = jnp.pad(in_full[:, main:], ((0, 0), (0, LANES - HEADS)))
    raw = jnp.dot(normed, tail, preferred_element_type=F32)
    grad_mixer = lax.dot_general(masked, out_full, NT, preferred_element_type=F32)
    pre, scanned, mixer_low = forward_mixer(projected, raw, small)
    grad_out_w = lax.dot_general(mixer_low, masked, TN, preferred_element_type=F32)
    out_share = lax.psum_scatter(
        grad_out_w.astype(BF16), "fsdp", scatter_dimension=0, tiled=True
    ).astype(F32)
    branch = jnp.dot(mixer_low, out_full, preferred_element_type=F32)
    output = (source + live_rows[:, None] * branch).astype(BF16)
    glow, graw, gconv, gdi, ghead = backward_mixer(projected, raw, small, pre, scanned, grad_mixer)
    grad_low = jnp.concatenate([glow, graw], axis=1)
    grad_in_w = lax.dot_general(normed, grad_low, TN, preferred_element_type=F32)
    in_share = lax.optimization_barrier(
        lax.psum_scatter(grad_in_w.astype(BF16), "fsdp", scatter_dimension=0, tiled=True)
    )[:, :proj_width].astype(F32)
    grad_normed = lax.dot_general(glow, in_full[:, :main], NT, preferred_element_type=F32)
    grad_normed = grad_normed + lax.dot_general(graw, tail, NT, preferred_element_type=F32)
    _, norm_vjp = jax.vjp(rms_scale, source, gain_norm)
    grad_source, grad_gain = norm_vjp(grad_normed)
    grad_input = out_cotangent.astype(F32) + grad_source
    skip_part = gdi[1].reshape(HEADS, HDIM).sum(axis=1)
    heads = jnp.concatenate([ghead[0, :HEADS], ghead[1, :HEADS], skip_part])
    rows = jnp.concatenate(
        [
            grad_gain.reshape(devices, -1),
            jnp.moveaxis(gconv[:KCONV].reshape(KCONV, devices, -1), 0, 1).reshape(devices, -1),
            gconv[KCONV].reshape(devices, -1),
            gdi[0].reshape(devices, -1),
            jnp.broadcast_to(heads, (devices, heads.shape[0])),
        ],
        axis=1,
    )
    cols = -(-rows.shape[1] // LANES) * LANES
    rows = jnp.pad(rows, ((0, 0), (0, cols - rows.shape[1])))
    mine = lax.psum_scatter(rows, "fsdp", scatter_dimension=0, tiled=True)[0]
    head_sums = mine[d : d + 3 * HEADS].reshape(3, HEADS)
    return (
        output,
        grad_input,
        mine[:a],
        in_share,
        mine[a:b].reshape(KCONV, -1).T,
        mine[b:c],
        head_sums[0],
        head_sums[1],
        head_sums[2],
        mine[c:d],
        out_share,
    )


def solution(mesh):
    rows, vec, whole = P("fsdp", None), P("fsdp"), P()
    in_specs = (rows, vec, vec, vec, rows, rows, vec, whole, whole, whole, vec, rows, rows)
    out_specs = (rows, rows, vec, rows, rows, vec, whole, whole, whole, vec, rows)
    return jax.shard_map(
        per_device, mesh=mesh, in_specs=in_specs, out_specs=out_specs, check_vma=False
    )
```

time: 643 us -> 483 us (0.75); the launches traced: 632 us -> 482 us
  waiting for transfers between devices: 203 us -> 381 us
  local copies, waits for them, and re-layouts: 158 us -> 29.7 us
  blocking collectives: 123 us -> 0 us
  matrix products: 70.3 us -> 20.5 us
  other arithmetic: 60.3 us -> 11.7 us
  Pallas kernels: 0 us -> 23.4 us
    reduce_scatter x0 -> x1, waiting for transfers between devices: none -> 101 us  [per_device(): lax.psum_scatter(grad_out_w.astype(BF16), 'fsdp', scatter_dimension=0, ti...]
    unnamed x2 -> x0, blocking collectives: 82.2 us -> none
    dynamic_update_slice x8 -> x0, local copies, waits for them, and re-layouts: 81.5 us -> none  [run_mixer(): _, outputs = lax.scan(jax.checkpoint(block_step), initial_state, pieces)]
    all_gather x2 -> x1, waiting for transfers between devices: 0.02 us -> 67.7 us  [per_device(): everything = lax.all_gather(packed, 'fsdp', axis=0, tiled=True)]
    dot_general x40 -> x8, matrix products: 70.3 us -> 20.5 us  [the longest x1 4.03 us: per_device(): lax.dot_general(normed, grad_low, TN, preferred_element_type=F32)]
    all_gather x1 -> x0, blocking collectives: 40.8 us -> none  [per_device(): lax.all_gather(conv_weight, 'fsdp', axis=0, tiled=True)]
    pallas_call x0 -> x2, Pallas kernels: none -> 23.4 us  [the longest x1 15.5 us: backward_mixer(): pl.pallas_call(backward_kernel, out_shape=(jax.ShapeDtypeStruct((length,...]
    reshape x12 -> x15, local copies, waits for them, and re-layouts: 29.1 us -> 9.54 us  [the longest x1 3.55 us: per_device(): everything[:, :fold].reshape(devices * out_weight.shape[0], width)]
  transfers between devices with their start and end apart: 3 -> 4, of which waited for: 1 -> 4; matrix products, arithmetic and copies ran while one was open for 17% -> 6% of each run, Pallas kernels for 0% -> 0%
where the time goes in v1:
time: 483 us; the launch traced here: 482 us
  waiting for transfers between devices  381 us (79%)
  local copies, waits for them, and re-layouts  29.7 us (6%)
  Pallas kernels  23.4 us (5%)
  matrix products  20.5 us (4%)
  between operations  14.7 us (3%)
  other arithmetic  11.7 us (2%)
    unnamed x6, waiting for transfers between devices  213 us
    reduce_scatter x1, waiting for transfers between devices, per_device(): lax.psum_scatter(grad_out_w.astype(BF16), 'fsdp', scatter_dimension=0, ti...  101 us
    all_gather x1, waiting for transfers between devices, per_device(): everything = lax.all_gather(packed, 'fsdp', axis=0, tiled=True)  67.7 us
    pallas_call x1, Pallas kernels, backward_mixer(): pl.pallas_call(backward_kernel, out_shape=(jax.ShapeDtypeStruct((length,...  15.5 us
  transfers between devices with their start and end apart: 4, of which 4 were waited for; matrix products, arithmetic and copies ran while one was open for 6% of the time, Pallas kernels for 0%

profile of v1, /device:TPU:0, one launch (start us, length us, event | category | flops | bytes accessed | tf_op | source)
XLA Modules:
  0.0 481.6 jit_solution(13823345888046733628)
XLA Ops:
  9.8 1.7 concatenate.31
  11.5 1.3 slice.116
  15.6 1.6 compare_and_fusion.2
  21.0 67.7 %all-gather.2.cloned.1.call-done = bf16[768,4992]{1,0:T(8,128)(2,1)} async-done(((bf16[24,4992]{1,0:T(8,128)(2,1)}), bf16[768,4992]{1,0:T(8,128)(2,1)}) %all-gather.2.cloned.1.call-update) | async-done | bytes 7667728 | tf_op jit(solution)/shard_map/all_gather | solution.py:333
  90.6 3.4 slice.150
  94.0 3.6 reshape.128
  99.1 1.8 fusion.18.gm_ref
  101.0 4.0 fusion.2.proj_ref
  105.0 7.9 %mixer_forward.1 = (f32[256,1792]{1,0:T(8,128)S(1)}, f32[256,1536]{1,0:T(8,128)S(1)}, bf16[256,1536]{1,0:T(8,128)(2,1)S(1)}) custom-call(f32[256,3328]{1,0:T(8,128)S(1)} %fusion.2.proj_ref, f32[256,128]{1,0:T(8,128)S(1)} %fusion.16.raw_ref, s32[256,1]{1,0:T(8,128)S(1)} %copy.35.segc_ref, s32[1,256]{1,0:T(1,128)S(1)} %bitcast.44, ...), custom_call_target="tpu_custom_call" | custom-call | flops 440401920 | bytes 7680000 | tf_op jit(solution)/shard_map/mixer_forward/pallas_call | solution.py:240
  112.9 15.5 %mixer_backward.1 = (bf16[256,3328]{1,0:T(8,128)(2,1)S(1)}, bf16[256,128]{1,0:T(8,128)(2,1)S(1)}, f32[8,1792]{1,0:T(8,128)S(1)}, f32[8,1536]{1,0:T(8,128)S(1)}, f32[8,128]{1,0:T(8,128)S(1)}) custom-call(f32[256,3328]{1,0:T(8,128)S(1)} %fusion.2.proj_ref, f32[256,128]{1,0:T(8,128)S(1)} %fusion.16.raw_ref, s32[256,1]{1,0:T(8,128)S(1)} %copy.35.segc_ref, ...), custom_call_target="tpu_custom_call" | custom-call | flops 1258291200 | bytes 15360000 | tf_op jit(solution)/shard_map/mixer_backward/pallas_call | solution.py:268
  131.0 4.0 fusion
  134.9 1.8 fusion.11
  141.0 3.0 convolution_convert_fusion.1
  144.2 4.0 convolution_convert_fusion
  148.9 2.4 fusion.12
  151.4 1.5 fusion.7
  152.9 106.1 %all-reduce.10.cloned.1.call-done = f32[32,512]{1,0:T(8,128)} async-done(((f32[32,512]{1,0:T(8,128)}), f32[32,512]{1,0:T(8,128)}) %all-reduce.10.cloned.1.call-update) | async-done | bytes 65552
  260.5 1.3 dynamic-slice_bitcast_fusion.4
  261.7 1.3 dynamic-slice_bitcast_fusion
  263.0 1.4 dynamic-slice_bitcast_fusion.1
  264.4 100.7 %reduce-scatter.5.cloned.1.call-done = bf16[48,768]{1,0:T(8,128)(2,1)} async-done(((bf16[1536,768]{1,0:T(8,128)(2,1)}), bf16[48,768]{1,0:T(8,128)(2,1)}) %reduce-scatter.5.cloned.1.call-update) | async-done | bytes 73744 | tf_op jit(solution)/shard_map/reduce_scatter | solution.py:380
  365.2 1.6 convert_element_type.64
  366.7 106.6 %reduce-scatter.7.cloned.1.call-done = bf16[24,3456]{1,0:T(8,128)(2,1)} async-done(((bf16[768,3456]{1,0:T(8,128)(2,1)}), bf16[24,3456]{1,0:T(8,128)(2,1)}) %reduce-scatter.7.cloned.1.call-update) | async-done | bytes 165904
  473.4 1.7 slice_convert_fusion.1
  (83 shorter events, 21.1 us)
Async XLA Ops:
  7.2 81.5 %all-gather.2.cloned.1.call-start = ((), (), s32[]{:S(2)}) async-start(), calls=%async_computation.2 | async-start | bytes 7907328 | tf_op jit(solution)/shard_map/all_gather | solution.py:333
  11.5 247.5 %all-reduce.10.cloned.1.call-start = ((), (), s32[]{:S(2)}) async-start(), calls=%async_computation.4 | async-start | bytes 131072
  19.1 80.0 %copy-start.8 = (pred[256]{0:T(512)(128)(4,1)}, pred[256]{0:T(512)(128)(4,1)S(1)}, u32[]{:S(2)}) copy-start(pred[256]{0:T(512)(128)(4,1)S(1)} %broadcast_compare_fusion) | copy-start | bytes 772
  21.0 69.1 %copy-start.5 = (f32[256]{0:T(256)}, f32[256]{0:T(256)S(1)}, u32[]{:S(2)}) copy-start(f32[256]{0:T(256)S(1)} %fusion.13) | copy-start | bytes 3076
  94.0 4.8 %copy-start.3 = (bf16[256,768]{1,0:T(8,128)(2,1)S(1)}, bf16[256,768]{1,0:T(8,128)(2,1)}, u32[]{:S(2)}) copy-start(bf16[256,768]{1,0:T(8,128)(2,1)} %param.13) | copy-start | bytes 1179652
  97.5 3.4 copy-start.1
  101.0 4.0 copy-start
  134.9 6.0 %copy-start.4 = (bf16[256,768]{1,0:T(8,128)(2,1)S(1)}, bf16[256,768]{1,0:T(8,128)(2,1)}, u32[]{:S(2)}) copy-start(bf16[256,768]{1,0:T(8,128)(2,1)} %param.25) | copy-start | bytes 1179652
  140.9 224.3 %reduce-scatter.5.cloned.1.call-start = ((), (), s32[]{:S(2)}) async-start(), calls=%async_computation.3 | async-start | bytes 2433024 | tf_op jit(solution)/shard_map/reduce_scatter | solution.py:380
  144.0 329.4 %reduce-scatter.7.cloned.1.call-start = ((), (), s32[]{:S(2)}) async-start(), calls=%async_computation.5 | async-start | bytes 5474304
  148.2 0.7 copy-start.6
  148.2 0.7 copy-start.7
  148.3 3.1 copy-start.2
Sparse Core Ops, SparseCore 0:
  11.6 76.9 all-gather.1
  141.0 117.9 all-reduce.9
  264.3 100.8 reduce-scatter.4
  370.7 102.5 reduce-scatter.6

commit v2 on v1

--- a/solution.py
+++ b/solution.py
@@ -20,6 +20,7 @@
 BF16 = jnp.bfloat16
 NT = (((1,), (1,)), ((), ()))
 TN = (((0,), (0,)), ((), ()))
+MESH = pl.DeviceIdType.MESH
 
 
 def rms_scale(values, gain_vec):
@@ -294,6 +295,204 @@
     )(proj, raw, *small, pre, scanned, grad_mixer)
 
 
+def pair_barrier(me, half):
+    core, chip = lax.rem(me, 2), lax.div(me, 2)
+    partner = me + 1 - 2 * core
+    barrier = pltpu.get_barrier_semaphore()
+    pl.semaphore_signal(barrier, inc=1, device_id=(partner,), device_id_type=MESH)
+
+    def greet(k, _):
+        other = 2 * lax.rem(chip + 1 + k, half) + core
+        pl.semaphore_signal(barrier, inc=1, device_id=(other,), device_id_type=MESH)
+        return 0
+
+    lax.fori_loop(0, half - 1, greet, 0)
+    pl.semaphore_wait(barrier, half)
+    return core, chip, partner
+
+
+def loop(count, step):
+    def body(k, _):
+        step(k)
+        return 0
+
+    lax.fori_loop(0, count, body, 0)
+
+
+def gather_kernel(
+    n, x0, x1, x2, o0, o1, o2, own_sem, send_far, recv_far, send_near, recv_near
+):
+    half = n // 2
+    me = lax.axis_index("fsdp")
+    core, chip, partner = pair_barrier(me, half)
+    groups = ((x0, o0), (x1, o1), (x2, o2))
+
+    def far(g, k, slot):
+        src, dst = groups[g]
+        return pltpu.make_async_remote_copy(
+            src_ref=src,
+            dst_ref=dst.at[slot],
+            send_sem=send_far.at[g, k],
+            recv_sem=recv_far.at[g, k],
+            device_id=(2 * lax.rem(chip + 1 + k, half) + core,),
+            device_id_type=MESH,
+        )
+
+    def near(g, k, src, slot):
+        return pltpu.make_async_remote_copy(
+            src_ref=src,
+            dst_ref=groups[g][1].at[slot],
+            send_sem=send_near.at[g, k],
+            recv_sem=recv_near.at[g, k],
+            device_id=(partner,),
+            device_id_type=MESH,
+        )
+
+    def origin(k):
+        return 2 * lax.rem(chip + half - 1 - k, half)
+
+    loop(half - 1, lambda k: [far(g, k, me).start() for g in range(3)] and None)
+    for g in range(3):
+        near(g, half - 1, groups[g][0], me).start()
+        pltpu.make_async_copy(groups[g][0], groups[g][1].at[me], own_sem.at[g]).start()
+
+    def forward(k):
+        slot = origin(k) + core
+        for g in range(3):
+            far(g, k, slot).wait_recv()
+            near(g, k, groups[g][1].at[slot], slot).start()
+
+    loop(half - 1, forward)
+
+    def drain(k):
+        slot, other = origin(k) + core, origin(k) + 1 - core
+        for g in range(3):
+            near(g, k, groups[g][1].at[slot], other).wait_recv()
+            near(g, k, groups[g][1].at[slot], slot).wait_send()
+            far(g, k, me).wait_send()
+
+    loop(half - 1, drain)
+    for g in range(3):
+        near(g, half - 1, groups[g][0], partner).wait_recv()
+        near(g, half - 1, groups[g][0], me).wait_send()
+        pltpu.make_async_copy(groups[g][0], groups[g][1].at[me], own_sem.at[g]).wait()
+
+
+def reduce_kernel(
+    n, a0, a1, a2, o0, o1, o2, p0, p1, p2, t0, t1, t2, q0, q1, q2,
+    send_near, recv_near, send_far, recv_far,
+):
+    half = n // 2
+    me = lax.axis_index("fsdp")
+    core, chip, partner = pair_barrier(me, half)
+    groups = ((a0, o0, p0, t0, q0), (a1, o1, p1, t1, q1), (a2, o2, p2, t2, q2))
+
+    def target(k):
+        return lax.rem(chip + 1 + k, half)
+
+    def near(g, k):
+        terms, _, got, _, _ = groups[g]
+        return pltpu.make_async_remote_copy(
+            src_ref=terms.at[2 * target(k) + 1 - core],
+            dst_ref=got.at[k],
+            send_sem=send_near.at[g, k],
+            recv_sem=recv_near.at[g, k],
+            device_id=(partner,),
+            device_id_type=MESH,
+        )
+
+    def far(g, k):
+        _, _, _, sums, got = groups[g]
+        return pltpu.make_async_remote_copy(
+            src_ref=sums.at[k],
+            dst_ref=got.at[k],
+            send_sem=send_far.at[g, k],
+            recv_sem=recv_far.at[g, k],
+            device_id=(2 * target(k) + core,),
+            device_id_type=MESH,
+        )
+
+    def both(g, k):
+        terms, _, got, _, _ = groups[g]
+        near(g, k).wait_recv()
+        return terms[2 * target(k) + core].astype(F32) + got[k].astype(F32)
+
+    loop(half, lambda k: [near(g, k).start() for g in range(3)] and None)
+
+    def pass_on(k):
+        for g in range(3):
+            sums = groups[g][3]
+            sums[k] = both(g, k).astype(sums.dtype)
+
+        @pl.when(k > 0)
+        def _():
+            for g in range(3):
+                far(g, k - 1).start()
+
+    loop(half - 1, pass_on)
+    for g in range(3):
+        groups[g][1][...] = both(g, half - 1)
+    for g in range(3):
+        far(g, half - 2).start()
+
+    def collect(k):
+        for g in range(3):
+            far(g, k).wait_recv()
+            groups[g][1][...] += groups[g][4][k].astype(F32)
+
+    loop(half - 1, collect)
+
+    def drain(k):
+        for g in range(3):
+            near(g, k).wait_send()
+
+    def drain_far(k):
+        for g in range(3):
+            far(g, k).wait_send()
+
+    loop(half, drain)
+    loop(half - 1, drain_far)
+
+
+def gather_all(n, shards):
+    vmem = pl.BlockSpec(memory_space=pltpu.VMEM)
+    half = n // 2
+    return pl.pallas_call(
+        functools.partial(gather_kernel, n),
+        out_shape=tuple(jax.ShapeDtypeStruct((n,) + x.shape, x.dtype) for x in shards),
+        in_specs=[vmem] * 3,
+        out_specs=[vmem] * 3,
+        scratch_shapes=[
+            pltpu.SemaphoreType.DMA((3,)),
+            pltpu.SemaphoreType.DMA((3, half)),
+            pltpu.SemaphoreType.DMA((3, half)),
+            pltpu.SemaphoreType.DMA((3, half)),
+            pltpu.SemaphoreType.DMA((3, half)),
+        ],
+        compiler_params=pltpu.CompilerParams(
+            collective_id=0, has_side_effects=True, vmem_limit_bytes=60 * 2**20
+        ),
+        name="gather_all",
+    )(*shards)
+
+
+def reduce_all(n, terms):
+    vmem = pl.BlockSpec(memory_space=pltpu.VMEM)
+    half = n // 2
+    slots = [pltpu.VMEM((half,) + x.shape[1:], x.dtype) for x in terms]
+    return pl.pallas_call(
+        functools.partial(reduce_kernel, n),
+        out_shape=tuple(jax.ShapeDtypeStruct(x.shape[1:], F32) for x in terms),
+        in_specs=[vmem] * 3,
+        out_specs=[vmem] * 3,
+        scratch_shapes=slots * 3 + [pltpu.SemaphoreType.DMA((3, half))] * 4,
+        compiler_params=pltpu.CompilerParams(
+            collective_id=1, has_side_effects=True, vmem_limit_bytes=60 * 2**20
+        ),
+        name="reduce_all",
+    )(*terms)
+
+
 def per_device(
     block_in,
     segment_ids,
@@ -316,24 +515,12 @@
     smalls = jnp.concatenate(
         [norm_gain, conv_weight.T.reshape(-1), conv_bias, gated_gain]
     )
-    small_cols = -(-smalls.shape[0] // share)
-    fold = out_weight.size // share
-    used = proj_width + fold + small_cols
-    padded = -(-used // LANES) * LANES
-    packed = jnp.concatenate(
-        [
-            out_weight.reshape(share, fold),
-            in_weight,
-            jnp.pad(smalls, (0, share * (padded - proj_width - fold) - smalls.shape[0])).reshape(
-                share, padded - proj_width - fold
-            ),
-        ],
-        axis=1,
-    )
-    everything = lax.all_gather(packed, "fsdp", axis=0, tiled=True)
-    in_full = everything[:, fold : fold + proj_width]
-    out_full = everything[:, :fold].reshape(devices * out_weight.shape[0], width)
-    rest = everything[:, fold + proj_width :].reshape(devices, -1).astype(F32)
+    small_rows = -(-smalls.shape[0] // (8 * LANES)) * 8
+    smalls = jnp.pad(smalls, (0, small_rows * LANES - smalls.shape[0])).reshape(small_rows, LANES)
+    in_blocks, out_blocks, rest = gather_all(devices, (in_weight, out_weight, smalls))
+    in_full = in_blocks.reshape(devices * share, proj_width)
+    out_full = out_blocks.reshape(devices * out_weight.shape[0], width)
+    rest = rest.reshape(devices, -1).astype(F32)
     a = norm_gain.shape[0]
     b = a + conv_weight.size
     c = b + conv_bias.shape[0]
@@ -377,17 +564,11 @@
     grad_mixer = lax.dot_general(masked, out_full, NT, preferred_element_type=F32)
     pre, scanned, mixer_low = forward_mixer(projected, raw, small)
     grad_out_w = lax.dot_general(mixer_low, masked, TN, preferred_element_type=F32)
-    out_share = lax.psum_scatter(
-        grad_out_w.astype(BF16), "fsdp", scatter_dimension=0, tiled=True
-    ).astype(F32)
     branch = jnp.dot(mixer_low, out_full, preferred_element_type=F32)
     output = (source + live_rows[:, None] * branch).astype(BF16)
     glow, graw, gconv, gdi, ghead = backward_mixer(projected, raw, small, pre, scanned, grad_mixer)
     grad_low = jnp.concatenate([glow, graw], axis=1)
     grad_in_w = lax.dot_general(normed, grad_low, TN, preferred_element_type=F32)
-    in_share = lax.optimization_barrier(
-        lax.psum_scatter(grad_in_w.astype(BF16), "fsdp", scatter_dimension=0, tiled=True)
-    )[:, :proj_width].astype(F32)
     grad_normed = lax.dot_general(glow, in_full[:, :main], NT, preferred_element_type=F32)
     grad_normed = grad_normed + lax.dot_general(graw, tail, NT, preferred_element_type=F32)
     _, norm_vjp = jax.vjp(rms_scale, source, gain_norm)
@@ -405,9 +586,18 @@
         ],
         axis=1,
     )
-    cols = -(-rows.shape[1] // LANES) * LANES
-    rows = jnp.pad(rows, ((0, 0), (0, cols - rows.shape[1])))
-    mine = lax.psum_scatter(rows, "fsdp", scatter_dimension=0, tiled=True)[0]
+    sum_rows = -(-rows.shape[1] // (8 * LANES)) * 8
+    rows = jnp.pad(rows, ((0, 0), (0, sum_rows * LANES - rows.shape[1])))
+    in_share, out_share, mine = reduce_all(
+        devices,
+        (
+            grad_in_w.astype(BF16).reshape(devices, share, -1),
+            grad_out_w.astype(BF16).reshape(devices, -1, width),
+            rows.reshape(devices, sum_rows, LANES),
+        ),
+    )
+    in_share = in_share[:, :proj_width]
+    mine = mine.reshape(-1)
     head_sums = mine[d : d + 3 * HEADS].reshape(3, HEADS)
     return (
         output,

time: 483 us -> 305 us (0.63)
  the two profiles are of different devices: /device:TPU:0 before, /device:TPU:15 now
where the time goes in v2:
time: 305 us; the launch traced here: 304 us
  Pallas kernels  244 us (80%)
  local copies, waits for them, and re-layouts  35.7 us (12%)
  matrix products  15.8 us (5%)
  other arithmetic  6.83 us (2%)
    pallas_call x1, Pallas kernels, gather_all(): pl.pallas_call(functools.partial(gather_kernel, n), out_shape=tuple((jax....  111 us
    pallas_call x1, Pallas kernels, reduce_all(): pl.pallas_call(functools.partial(reduce_kernel, n), out_shape=tuple((jax....  109 us
    pallas_call x1, Pallas kernels, backward_mixer(): pl.pallas_call(backward_kernel, out_shape=(jax.ShapeDtypeStruct((length,...  15.6 us
    unnamed x57, local copies, waits for them, and re-layouts  10.1 us
    pallas_call x1, Pallas kernels, forward_mixer(): pl.pallas_call(forward_kernel, out_shape=(jax.ShapeDtypeStruct((length, C...  7.9 us

profile of v2, /device:TPU:15, one launch (start us, length us, event | category | flops | bytes accessed | tf_op | source)
XLA Modules:
  0.0 303.8 jit_solution(17067475906353882271)
XLA Ops:
  1.4 1.3 fusion.26.x2
  2.8 110.8 %gather_all.1 = (bf16[32,24,3352]{2,1,0:T(8,128)(2,1)}, bf16[32,48,768]{2,1,0:T(8,128)(2,1)}, bf16[32,8,128]{2,1,0:T(8,128)(2,1)}) custom-call(bf16[24,3352]{1,0:T(8,128)(2,1)} %x0.1, bf16[48,768]{1,0:T(8,128)(2,1)} %x1.1, bf16[8,128]{1,0:T(8,128)(2,1)} %fusion.26.x2), custom_call_target="tpu_custom_call" | custom-call | tf_op jit(solution)/shard_map/gather_all/pallas_call | solution.py:460
  114.6 1.2 fusion.13
  116.3 4.2 %fusion.2.proj_ref = f32[256,3328]{1,0:T(8,128)S(1)} fusion(bf16[768,3352]{1,0:T(8,128)(2,1)} %bitcast.62, bf16[256,768]{1,0:T(8,128)(2,1)} %param.13, f32[768]{0:T(1024)S(1)} %mul.75, f32[256]{0:T(256)S(1)} %fusion.27), kind=kOutput, calls=%fused_computation.3 | convolution fusion | flops 1309409280 | bytes 8916992 | tf_op jit(solution)/shard_map/dot_general | solution.py:561
  127.9 1.5 slice.121
  129.3 1.5 reshape.127
  130.8 1.5 copy.43
  132.3 1.5 reshape.128
  133.9 1.5 maximum_maximum_fusion.cw_ref
  136.0 1.2 pad_bitcast_fusion.1
  137.2 1.3 broadcast_in_dim.28
  139.3 1.4 slice.123
  146.1 7.9 %mixer_forward.1 = (f32[256,1792]{1,0:T(8,128)S(1)}, f32[256,1536]{1,0:T(8,128)S(1)}, bf16[256,1536]{1,0:T(8,128)(2,1)S(1)}) custom-call(f32[256,3328]{1,0:T(8,128)S(1)} %fusion.2.proj_ref, f32[256,128]{1,0:T(8,128)S(1)} %copy-done.1, s32[256,1]{1,0:T(8,128)S(1)} %copy-done, s32[1,256]{1,0:T(1,128)S(1)} %bitcast.47, f32[256,8]{1,0:T(8,128)S(1)} %pad_convert_fusion.shift_ref, ...), custom_call_target="tpu_custom_call" | custom-call | flops 440401920 | bytes 7680000 | tf_op jit(solution)/shard_map/mixer_forward/pallas_call | solution.py:241
  154.8 1.5 fusion.7
  157.2 15.6 %mixer_backward.1 = (bf16[256,3328]{1,0:T(8,128)(2,1)S(1)}, bf16[256,128]{1,0:T(8,128)(2,1)S(1)}, f32[8,1792]{1,0:T(8,128)S(1)}, f32[8,1536]{1,0:T(8,128)S(1)}, f32[8,128]{1,0:T(8,128)S(1)}) custom-call(f32[256,3328]{1,0:T(8,128)S(1)} %fusion.2.proj_ref, f32[256,128]{1,0:T(8,128)S(1)} %copy-done.1, s32[256,1]{1,0:T(8,128)S(1)} %copy-done, ...), custom_call_target="tpu_custom_call" | custom-call | flops 1258291200 | bytes 15360000 | tf_op jit(solution)/shard_map/mixer_backward/pallas_call | solution.py:269
  172.8 1.5 fusion
  176.1 4.1 %convolution_convert_fusion = bf16[768,3456]{1,0:T(8,128)(2,1)} fusion(bf16[256,128]{1,0:T(8,128)(2,1)S(1)} %get-tuple-element.32, bf16[256,3328]{1,0:T(8,128)(2,1)S(1)} %get-tuple-element.31, bf16[256,768]{1,0:T(8,128)(2,1)S(1)} %copy-done.12, f32[768]{0:T(1024)S(1)} %copy-done.19, f32[256]{0:T(256)S(1)} %copy-done.21), kind=kOutput, calls=%fused_computation | convolution fusion | flops 1365934080 | bytes 7475200 | tf_op jit(solution)/shard_map/dot_general | solution.py:571
  180.1 2.3 convolution_convert_fusion.1
  185.7 109.4 %reduce_all.1 = (f32[24,3456]{1,0:T(8,128)}, f32[48,768]{1,0:T(8,128)}, f32[8,128]{1,0:T(8,128)}) custom-call(bf16[32,24,3456]{2,1,0:T(8,128)(2,1)} %bitcast.49, bf16[32,48,768]{2,1,0:T(8,128)(2,1)} %bitcast.50, f32[32,8,128]{2,1,0:T(8,128)} %bitcast.53), custom_call_target="tpu_custom_call" | custom-call | tf_op jit(solution)/shard_map/reduce_all/pallas_call | solution.py:483
  295.1 1.4 fusion.36
  298.0 1.3 slice.113
  299.2 1.3 slice.117
  300.5 1.7 copy.47
  302.2 1.6 copy.48
  (102 shorter events, 23.7 us)
Async XLA Ops:
  114.4 1.3 copy-start.17
  114.6 6.9 %copy-start.18 = (f32[768]{0:T(1024)}, f32[768]{0:T(1024)S(1)}, u32[]{:S(2)}) copy-start(f32[768]{0:T(1024)S(1)} %mul.75) | copy-start | bytes 9220
  116.3 5.1 %copy-start.20 = (f32[256]{0:T(256)}, f32[256]{0:T(256)S(1)}, u32[]{:S(2)}) copy-start(f32[256]{0:T(256)S(1)} %fusion.27) | copy-start | bytes 3076
  116.3 5.1 %copy-start.11 = (bf16[256,768]{1,0:T(8,128)(2,1)S(1)}, bf16[256,768]{1,0:T(8,128)(2,1)}, u32[]{:S(2)}) copy-start(bf16[256,768]{1,0:T(8,128)(2,1)} %param.13) | copy-start | bytes 1179652
  116.3 6.1 %copy-start.3 = (s32[256]{0:T(256)S(1)}, s32[256]{0:T(256)}, u32[]{:S(2)}) copy-start(s32[256]{0:T(256)} %param.14) | copy-start | bytes 3076
  121.5 1.0 copy-start.15
  141.5 0.9 copy-start
  142.4 0.9 copy-start.1
  143.3 0.8 copy-start.2
  144.2 0.7 copy-start.4
  145.5 0.7 copy-start.8
  146.1 8.6 %copy-start.12 = (bf16[256,768]{1,0:T(8,128)(2,1)S(1)}, bf16[256,768]{1,0:T(8,128)(2,1)}, u32[]{:S(2)}) copy-start(bf16[256,768]{1,0:T(8,128)(2,1)} %param.13) | copy-start | bytes 1179652
  146.1 8.6 %copy-start.14 = (bf16[32,48,768]{2,1,0:T(8,128)(2,1)S(1)}, bf16[32,48,768]{2,1,0:T(8,128)(2,1)}, u32[]{:S(2)}) copy-start(bf16[32,48,768]{2,1,0:T(8,128)(2,1)} %get-tuple-element.28) | copy-start | bytes 7077892
  154.1 2.3 copy-start.13
  156.3 16.4 %slice-start = ((s8[5308416]{0:T(1024)(128)(4,1)}), s8[4194304]{0:T(1024)(128)(4,1)S(1)}, s32[]{:S(2)}) async-start(s8[5308416]{0:T(1024)(128)(4,1)} %bitcast.64), calls=%async_computation | async-start | bytes 8388608
  157.2 15.6 %slice-start.1 = ((s8[5308416]{0:T(1024)(128)(4,1)}), s8[1114112]{0:T(1024)(128)(4,1)S(1)}, s32[]{:S(2)}) async-start(s8[5308416]{0:T(1024)(128)(4,1)} %bitcast.64), calls=%async_computation.1 | async-start | bytes 2228224
  172.7 1.6 copy-start.5
  172.7 1.6 copy-start.9
  172.7 1.6 copy-start.10
  172.8 1.6 copy-start.16
  172.8 1.6 copy-start.19
  172.8 1.6 copy-start.21
  172.8 2.1 copy-start.23
  180.1 2.4 copy-start.6
  (2 other events, 1.2 us)

commit v3 on v2

--- a/solution.py
+++ b/solution.py
@@ -295,20 +295,17 @@
     )(proj, raw, *small, pre, scanned, grad_mixer)
 
 
-def pair_barrier(me, half):
+def place(n):
+    me = lax.axis_index("fsdp")
     core, chip = lax.rem(me, 2), lax.div(me, 2)
-    partner = me + 1 - 2 * core
-    barrier = pltpu.get_barrier_semaphore()
-    pl.semaphore_signal(barrier, inc=1, device_id=(partner,), device_id_type=MESH)
-
-    def greet(k, _):
-        other = 2 * lax.rem(chip + 1 + k, half) + core
-        pl.semaphore_signal(barrier, inc=1, device_id=(other,), device_id_type=MESH)
-        return 0
-
-    lax.fori_loop(0, half - 1, greet, 0)
-    pl.semaphore_wait(barrier, half)
-    return core, chip, partner
+    plane, line = split(n)
+    return me, core, lax.rem(chip, plane), lax.div(chip, plane)
+
+
+def split(n):
+    half = n // 2
+    plane = 4 if half % 4 == 0 else 1
+    return plane, half // plane
 
 
 def loop(count, step):
@@ -319,144 +316,222 @@
     lax.fori_loop(0, count, body, 0)
 
 
+def greet(n, me, core, spot, rank):
+    plane, line = split(n)
+    barrier = pltpu.get_barrier_semaphore()
+
+    def signal(device):
+        pl.semaphore_signal(barrier, inc=1, device_id=(device,), device_id_type=MESH)
+
+    signal(me + 1 - 2 * core)
+    for j in range(plane - 1):
+        signal(2 * (rank * plane + lax.rem(spot + 1 + j, plane)) + core)
+    loop(line - 1, lambda r: signal(2 * (lax.rem(rank + 1 + r, line) * plane + spot) + core))
+    pl.semaphore_wait(barrier, plane + line - 1)
+
+
 def gather_kernel(
-    n, x0, x1, x2, o0, o1, o2, own_sem, send_far, recv_far, send_near, recv_near
+    n, x0, x1, x2, o0, o1, o2, own_sem, s_line, r_line, s_plane, r_plane, s_near, r_near
 ):
-    half = n // 2
-    me = lax.axis_index("fsdp")
-    core, chip, partner = pair_barrier(me, half)
+    plane, line = split(n)
+    me, core, spot, rank = place(n)
+    partner = me + 1 - 2 * core
+    greet(n, me, core, spot, rank)
     groups = ((x0, o0), (x1, o1), (x2, o2))
 
-    def far(g, k, slot):
-        src, dst = groups[g]
-        return pltpu.make_async_remote_copy(
-            src_ref=src,
-            dst_ref=dst.at[slot],
-            send_sem=send_far.at[g, k],
-            recv_sem=recv_far.at[g, k],
-            device_id=(2 * lax.rem(chip + 1 + k, half) + core,),
-            device_id_type=MESH,
-        )
-
-    def near(g, k, src, slot):
+    def send(g, src, slot, sems, index, device):
         return pltpu.make_async_remote_copy(
             src_ref=src,
             dst_ref=groups[g][1].at[slot],
-            send_sem=send_near.at[g, k],
-            recv_sem=recv_near.at[g, k],
-            device_id=(partner,),
+            send_sem=sems[0].at[g, index],
+            recv_sem=sems[1].at[g, index],
+            device_id=(device,),
             device_id_type=MESH,
         )
 
-    def origin(k):
-        return 2 * lax.rem(chip + half - 1 - k, half)
-
-    loop(half - 1, lambda k: [far(g, k, me).start() for g in range(3)] and None)
+    def origin(r, j):
+        from_rank = lax.rem(rank + 2 * line - 1 - r, line)
+        return 2 * (from_rank * plane + lax.rem(spot + 2 * plane - 1 - j, plane))
+
+    def along(g, r, slot):
+        device = 2 * (lax.rem(rank + 1 + r, line) * plane + spot) + core
+        return send(g, groups[g][0], slot, (s_line, r_line), r, device)
+
+    def across(g, r, j, src, slot):
+        device = 2 * (rank * plane + lax.rem(spot + 1 + j, plane)) + core
+        return send(g, src, slot, (s_plane, r_plane), plane * r + j, device)
+
+    def near(g, r, j, src, slot):
+        return send(g, src, slot, (s_near, r_near), plane * r + j, partner)
+
+    def start_along(r):
+        for g in range(3):
+            along(g, r, me).start()
+
+    loop(line - 1, start_along)
     for g in range(3):
-        near(g, half - 1, groups[g][0], me).start()
-        pltpu.make_async_copy(groups[g][0], groups[g][1].at[me], own_sem.at[g]).start()
-
-    def forward(k):
-        slot = origin(k) + core
+        x = groups[g][0]
+        for j in range(plane - 1):
+            across(g, line - 1, j, x, me).start()
+        near(g, line - 1, plane - 1, x, me).start()
+        pltpu.make_async_copy(x, groups[g][1].at[me], own_sem.at[g]).start()
+
+    def forward(r):
+        for j in range(plane - 1):
+            slot = origin(r, j) + core
+            for g in range(3):
+                block = groups[g][1].at[slot]
+                across(g, r, j, block, slot).wait_recv()
+                near(g, r, j, block, slot).start()
+
+    def spread(r):
+        slot = origin(r, plane - 1) + core
         for g in range(3):
-            far(g, k, slot).wait_recv()
-            near(g, k, groups[g][1].at[slot], slot).start()
-
-    loop(half - 1, forward)
-
-    def drain(k):
-        slot, other = origin(k) + core, origin(k) + 1 - core
+            block = groups[g][1].at[slot]
+            along(g, r, slot).wait_recv()
+            for j in range(plane - 1):
+                across(g, r, j, block, slot).start()
+            near(g, r, plane - 1, block, slot).start()
+        forward(lax.rem(r + line - 1, line))
+
+    loop(line - 1, spread)
+    forward((line - 2) % line)
+
+    def drain(r):
+        for j in range(plane):
+            slot, other = origin(r, j) + core, origin(r, j) + 1 - core
+            for g in range(3):
+                block = groups[g][1].at[slot]
+                near(g, r, j, block, other).wait_recv()
+                near(g, r, j, block, slot).wait_send()
+                if j < plane - 1:
+                    across(g, r, j, block, slot).wait_send()
+
+    loop(line, drain)
+
+    def drain_along(r):
         for g in range(3):
-            near(g, k, groups[g][1].at[slot], other).wait_recv()
-            near(g, k, groups[g][1].at[slot], slot).wait_send()
-            far(g, k, me).wait_send()
-
-    loop(half - 1, drain)
+            along(g, r, me).wait_send()
+
+    loop(line - 1, drain_along)
     for g in range(3):
-        near(g, half - 1, groups[g][0], partner).wait_recv()
-        near(g, half - 1, groups[g][0], me).wait_send()
         pltpu.make_async_copy(groups[g][0], groups[g][1].at[me], own_sem.at[g]).wait()
 
 
 def reduce_kernel(
     n, a0, a1, a2, o0, o1, o2, p0, p1, p2, t0, t1, t2, q0, q1, q2,
-    send_near, recv_near, send_far, recv_far,
+    u0, u1, u2, v0, v1, v2, w0, w1, w2,
+    s_near, r_near, s_plane, r_plane, s_line, r_line,
 ):
-    half = n // 2
-    me = lax.axis_index("fsdp")
-    core, chip, partner = pair_barrier(me, half)
-    groups = ((a0, o0, p0, t0, q0), (a1, o1, p1, t1, q1), (a2, o2, p2, t2, q2))
-
-    def target(k):
-        return lax.rem(chip + 1 + k, half)
-
-    def near(g, k):
-        terms, _, got, _, _ = groups[g]
+    plane, line = split(n)
+    me, core, spot, rank = place(n)
+    partner = me + 1 - 2 * core
+    greet(n, me, core, spot, rank)
+    groups = (
+        (a0, o0, p0, t0, q0, u0, v0, w0),
+        (a1, o1, p1, t1, q1, u1, v1, w1),
+        (a2, o2, p2, t2, q2, u2, v2, w2),
+    )
+
+    def send(src, dst, sems, g, index, device):
         return pltpu.make_async_remote_copy(
-            src_ref=terms.at[2 * target(k) + 1 - core],
-            dst_ref=got.at[k],
-            send_sem=send_near.at[g, k],
-            recv_sem=recv_near.at[g, k],
-            device_id=(partner,),
+            src_ref=src.at[index] if not isinstance(src, tuple) else src[0].at[src[1]],
+            dst_ref=dst.at[index],
+            send_sem=sems[0].at[g, index],
+            recv_sem=sems[1].at[g, index],
+            device_id=(device,),
             device_id_type=MESH,
         )
 
-    def far(g, k):
-        _, _, _, sums, got = groups[g]
-        return pltpu.make_async_remote_copy(
-            src_ref=sums.at[k],
-            dst_ref=got.at[k],
-            send_sem=send_far.at[g, k],
-            recv_sem=recv_far.at[g, k],
-            device_id=(2 * target(k) + core,),
-            device_id_type=MESH,
-        )
-
-    def both(g, k):
-        terms, _, got, _, _ = groups[g]
-        near(g, k).wait_recv()
-        return terms[2 * target(k) + core].astype(F32) + got[k].astype(F32)
-
-    loop(half, lambda k: [near(g, k).start() for g in range(3)] and None)
-
-    def pass_on(k):
+    def owner(r, j):
+        return 2 * (lax.rem(rank + 1 + r, line) * plane + lax.rem(spot + 1 + j, plane))
+
+    def near(g, r, j):
+        src = (groups[g][0], owner(r, j) + 1 - core)
+        return send(src, groups[g][2], (s_near, r_near), g, plane * r + j, partner)
+
+    def across(g, r, j):
+        device = 2 * (rank * plane + lax.rem(spot + 1 + j, plane)) + core
+        return send(groups[g][3], groups[g][4], (s_plane, r_plane), g, plane * r + j, device)
+
+    def along(g, r):
+        device = 2 * (lax.rem(rank + 1 + r, line) * plane + spot) + core
+        return send(groups[g][6], groups[g][7], (s_line, r_line), g, r, device)
+
+    def both(g, r, j):
+        near(g, r, j).wait_recv()
+        return groups[g][0][owner(r, j) + core].astype(F32) + groups[g][2][plane * r + j].astype(F32)
+
+    def start_near(r):
+        for j in range(plane):
+            for g in range(3):
+                near(g, r, j).start()
+
+    loop(line, start_near)
+
+    def pairs(r):
+        for j in range(plane):
+            for g in range(3):
+                if j < plane - 1:
+                    sums = groups[g][3]
+                    sums[plane * r + j] = both(g, r, j).astype(sums.dtype)
+                else:
+                    groups[g][5][r] = both(g, r, j)
+            if j > 0:
+                for g in range(3):
+                    across(g, r, j - 1).start()
+
+    def total(g, r):
+        result = groups[g][5][r]
+        for j in range(plane - 1):
+            across(g, r, j).wait_recv()
+            result = result + groups[g][4][plane * r + j].astype(F32)
+        return result
+
+    def planes(r):
         for g in range(3):
-            sums = groups[g][3]
-            sums[k] = both(g, k).astype(sums.dtype)
-
-        @pl.when(k > 0)
+            sums = groups[g][6]
+            sums[r] = total(g, r).astype(sums.dtype)
+        for g in range(3):
+            along(g, r).start()
+
+    def step(r):
+        pairs(r)
+
+        @pl.when(r > 0)
         def _():
-            for g in range(3):
-                far(g, k - 1).start()
-
-    loop(half - 1, pass_on)
+            planes(r - 1)
+
+    loop(line, step)
     for g in range(3):
-        groups[g][1][...] = both(g, half - 1)
-    for g in range(3):
-        far(g, half - 2).start()
-
-    def collect(k):
+        groups[g][1][...] = total(g, line - 1)
+
+    def collect(r):
         for g in range(3):
-            far(g, k).wait_recv()
-            groups[g][1][...] += groups[g][4][k].astype(F32)
-
-    loop(half - 1, collect)
-
-    def drain(k):
+            along(g, r).wait_recv()
+            groups[g][1][...] += groups[g][7][r].astype(F32)
+
+    loop(line - 1, collect)
+
+    def drain(r):
         for g in range(3):
-            near(g, k).wait_send()
-
-    def drain_far(k):
+            for j in range(plane):
+                near(g, r, j).wait_send()
+                if j < plane - 1:
+                    across(g, r, j).wait_send()
+
+    loop(line, drain)
+
+    def drain_along(r):
         for g in range(3):
-            far(g, k).wait_send()
-
-    loop(half, drain)
-    loop(half - 1, drain_far)
+            along(g, r).wait_send()
+
+    loop(line - 1, drain_along)
 
 
 def gather_all(n, shards):
     vmem = pl.BlockSpec(memory_space=pltpu.VMEM)
-    half = n // 2
+    half, (_, line) = n // 2, split(n)
     return pl.pallas_call(
         functools.partial(gather_kernel, n),
         out_shape=tuple(jax.ShapeDtypeStruct((n,) + x.shape, x.dtype) for x in shards),
@@ -464,6 +539,8 @@
         out_specs=[vmem] * 3,
         scratch_shapes=[
             pltpu.SemaphoreType.DMA((3,)),
+            pltpu.SemaphoreType.DMA((3, line)),
+            pltpu.SemaphoreType.DMA((3, line)),
             pltpu.SemaphoreType.DMA((3, half)),
             pltpu.SemaphoreType.DMA((3, half)),
             pltpu.SemaphoreType.DMA((3, half)),
@@ -478,14 +555,20 @@
 
 def reduce_all(n, terms):
     vmem = pl.BlockSpec(memory_space=pltpu.VMEM)
-    half = n // 2
+    half, (_, line) = n // 2, split(n)
     slots = [pltpu.VMEM((half,) + x.shape[1:], x.dtype) for x in terms]
+    partial_sums = [pltpu.VMEM((line,) + x.shape[1:], F32) for x in terms]
+    lines = [pltpu.VMEM((line,) + x.shape[1:], x.dtype) for x in terms]
     return pl.pallas_call(
         functools.partial(reduce_kernel, n),
         out_shape=tuple(jax.ShapeDtypeStruct(x.shape[1:], F32) for x in terms),
         in_specs=[vmem] * 3,
         out_specs=[vmem] * 3,
-        scratch_shapes=slots * 3 + [pltpu.SemaphoreType.DMA((3, half))] * 4,
+        scratch_shapes=slots * 3
+        + partial_sums
+        + lines * 2
+        + [pltpu.SemaphoreType.DMA((3, half))] * 4
+        + [pltpu.SemaphoreType.DMA((3, line))] * 2,
         compiler_params=pltpu.CompilerParams(
             collective_id=1, has_side_effects=True, vmem_limit_bytes=60 * 2**20
         ),

time: 305 us -> 195 us (0.64)
  the two profiles are of different devices: /device:TPU:15 before, /device:TPU:0 now
where the time goes in v3:
time: 195 us; the launch traced here: 194 us
  Pallas kernels  134 us (69%)
  local copies, waits for them, and re-layouts  35.7 us (18%)
  matrix products  15.8 us (8%)
  other arithmetic  6.83 us (4%)
    pallas_call x1, Pallas kernels, gather_all(): pl.pallas_call(functools.partial(gather_kernel, n), out_shape=tuple((jax....  56.9 us
    pallas_call x1, Pallas kernels, reduce_all(): pl.pallas_call(functools.partial(reduce_kernel, n), out_shape=tuple((jax....  53.2 us
    pallas_call x1, Pallas kernels, backward_mixer(): pl.pallas_call(backward_kernel, out_shape=(jax.ShapeDtypeStruct((length,...  15.6 us
    unnamed x57, local copies, waits for them, and re-layouts  10.1 us
    pallas_call x1, Pallas kernels, forward_mixer(): pl.pallas_call(forward_kernel, out_shape=(jax.ShapeDtypeStruct((length, C...  7.9 us
    dot_general x1, matrix products, per_device(): projected = jnp.dot(normed, in_full[:, :main], preferred_element_type=F32)  4.16 us
    dot_general x1, matrix products, per_device(): lax.dot_general(normed, grad_low, TN, preferred_element_type=F32)  4.07 us

profile of v3, /device:TPU:0, one launch (start us, length us, event | category | flops | bytes accessed | tf_op | source)
XLA Modules:
  0.0 193.7 jit_solution(8797045697234838975)
XLA Ops:
  1.4 1.3 fusion.26.x2
  2.8 56.9 %gather_all.1 = (bf16[32,24,3352]{2,1,0:T(8,128)(2,1)}, bf16[32,48,768]{2,1,0:T(8,128)(2,1)}, bf16[32,8,128]{2,1,0:T(8,128)(2,1)}) custom-call(bf16[24,3352]{1,0:T(8,128)(2,1)} %x0.1, bf16[48,768]{1,0:T(8,128)(2,1)} %x1.1, bf16[8,128]{1,0:T(8,128)(2,1)} %fusion.26.x2), custom_call_target="tpu_custom_call" | custom-call | tf_op jit(solution)/shard_map/gather_all/pallas_call | solution.py:535
  60.7 1.2 fusion.13
  62.4 4.2 %fusion.2.proj_ref = f32[256,3328]{1,0:T(8,128)S(1)} fusion(bf16[768,3352]{1,0:T(8,128)(2,1)} %bitcast.62, bf16[256,768]{1,0:T(8,128)(2,1)} %param.13, f32[768]{0:T(1024)S(1)} %mul.75, f32[256]{0:T(256)S(1)} %fusion.27), kind=kOutput, calls=%fused_computation.3 | convolution fusion | flops 1309409280 | bytes 8916992 | tf_op jit(solution)/shard_map/dot_general | solution.py:644
  73.9 1.5 slice.121
  75.4 1.5 reshape.127
  76.9 1.5 copy.43
  78.4 1.5 reshape.128
  80.0 1.5 maximum_maximum_fusion.cw_ref
  82.1 1.2 pad_bitcast_fusion.1
  83.3 1.3 broadcast_in_dim.28
  85.4 1.4 slice.123
  92.2 7.9 %mixer_forward.1 = (f32[256,1792]{1,0:T(8,128)S(1)}, f32[256,1536]{1,0:T(8,128)S(1)}, bf16[256,1536]{1,0:T(8,128)(2,1)S(1)}) custom-call(f32[256,3328]{1,0:T(8,128)S(1)} %fusion.2.proj_ref, f32[256,128]{1,0:T(8,128)S(1)} %copy-done.1, s32[256,1]{1,0:T(8,128)S(1)} %copy-done, s32[1,256]{1,0:T(1,128)S(1)} %bitcast.47, f32[256,8]{1,0:T(8,128)S(1)} %pad_convert_fusion.shift_ref, ...), custom_call_target="tpu_custom_call" | custom-call | flops 440401920 | bytes 7680000 | tf_op jit(solution)/shard_map/mixer_forward/pallas_call | solution.py:241
  100.9 1.5 fusion.7
  103.2 15.6 %mixer_backward.1 = (bf16[256,3328]{1,0:T(8,128)(2,1)S(1)}, bf16[256,128]{1,0:T(8,128)(2,1)S(1)}, f32[8,1792]{1,0:T(8,128)S(1)}, f32[8,1536]{1,0:T(8,128)S(1)}, f32[8,128]{1,0:T(8,128)S(1)}) custom-call(f32[256,3328]{1,0:T(8,128)S(1)} %fusion.2.proj_ref, f32[256,128]{1,0:T(8,128)S(1)} %copy-done.1, s32[256,1]{1,0:T(8,128)S(1)} %copy-done, ...), custom_call_target="tpu_custom_call" | custom-call | flops 1258291200 | bytes 15360000 | tf_op jit(solution)/shard_map/mixer_backward/pallas_call | solution.py:269
  118.9 1.5 fusion
  122.1 4.1 %convolution_convert_fusion = bf16[768,3456]{1,0:T(8,128)(2,1)} fusion(bf16[256,128]{1,0:T(8,128)(2,1)S(1)} %get-tuple-element.32, bf16[256,3328]{1,0:T(8,128)(2,1)S(1)} %get-tuple-element.31, bf16[256,768]{1,0:T(8,128)(2,1)S(1)} %copy-done.12, f32[768]{0:T(1024)S(1)} %copy-done.19, f32[256]{0:T(256)S(1)} %copy-done.21), kind=kOutput, calls=%fused_computation | convolution fusion | flops 1365934080 | bytes 7475200 | tf_op jit(solution)/shard_map/dot_general | solution.py:654
  126.2 2.3 %convolution_convert_fusion.1 = bf16[1536,768]{1,0:T(8,128)(2,1)} fusion(bf16[256,1536]{1,0:T(8,128)(2,1)S(1)} %get-tuple-element.27, bf16[256,768]{1,0:T(8,128)(2,1)S(1)} %copy-done.13, pred[256]{0:T(512)(128)(4,1)S(1)} %get-tuple-element.56), kind=kOutput, calls=%fused_computation.5 | convolution fusion | flops 605356032 | bytes 3539200 | tf_op jit(solution)/shard_map/dot_general | solution.py:649
  131.8 53.2 %reduce_all.1 = (f32[24,3456]{1,0:T(8,128)}, f32[48,768]{1,0:T(8,128)}, f32[8,128]{1,0:T(8,128)}) custom-call(bf16[32,24,3456]{2,1,0:T(8,128)(2,1)} %bitcast.49, bf16[32,48,768]{2,1,0:T(8,128)(2,1)} %bitcast.50, f32[32,8,128]{2,1,0:T(8,128)} %bitcast.53), custom_call_target="tpu_custom_call" | custom-call | tf_op jit(solution)/shard_map/reduce_all/pallas_call | solution.py:562
  185.1 1.4 fusion.36
  187.9 1.3 slice.113
  189.2 1.3 slice.117
  190.4 1.7 copy.47
  192.1 1.6 copy.48
  (102 shorter events, 23.7 us)
Async XLA Ops:
  60.5 1.3 copy-start.17
  60.6 6.9 %copy-start.18 = (f32[768]{0:T(1024)}, f32[768]{0:T(1024)S(1)}, u32[]{:S(2)}) copy-start(f32[768]{0:T(1024)S(1)} %mul.75) | copy-start | bytes 9220
  62.4 5.1 %copy-start.20 = (f32[256]{0:T(256)}, f32[256]{0:T(256)S(1)}, u32[]{:S(2)}) copy-start(f32[256]{0:T(256)S(1)} %fusion.27) | copy-start | bytes 3076
  62.4 5.1 %copy-start.11 = (bf16[256,768]{1,0:T(8,128)(2,1)S(1)}, bf16[256,768]{1,0:T(8,128)(2,1)}, u32[]{:S(2)}) copy-start(bf16[256,768]{1,0:T(8,128)(2,1)} %param.13) | copy-start | bytes 1179652
  62.4 6.1 %copy-start.3 = (s32[256]{0:T(256)S(1)}, s32[256]{0:T(256)}, u32[]{:S(2)}) copy-start(s32[256]{0:T(256)} %param.14) | copy-start | bytes 3076
  67.6 1.0 copy-start.15
  87.6 0.9 copy-start
  88.5 0.9 copy-start.1
  89.4 0.8 copy-start.2
  90.2 0.7 copy-start.4
  90.9 0.7 copy-start.7
  92.2 8.6 %copy-start.12 = (bf16[256,768]{1,0:T(8,128)(2,1)S(1)}, bf16[256,768]{1,0:T(8,128)(2,1)}, u32[]{:S(2)}) copy-start(bf16[256,768]{1,0:T(8,128)(2,1)} %param.13) | copy-start | bytes 1179652
  92.2 8.6 %copy-start.14 = (bf16[32,48,768]{2,1,0:T(8,128)(2,1)S(1)}, bf16[32,48,768]{2,1,0:T(8,128)(2,1)}, u32[]{:S(2)}) copy-start(bf16[32,48,768]{2,1,0:T(8,128)(2,1)} %get-tuple-element.28) | copy-start | bytes 7077892
  100.1 2.3 %copy-start.13 = (bf16[256,768]{1,0:T(8,128)(2,1)S(1)}, bf16[256,768]{1,0:T(8,128)(2,1)}, u32[]{:S(2)}) copy-start(bf16[256,768]{1,0:T(8,128)(2,1)} %param.25) | copy-start | bytes 1179652
  102.4 16.4 %slice-start = ((s8[5308416]{0:T(1024)(128)(4,1)}), s8[4194304]{0:T(1024)(128)(4,1)S(1)}, s32[]{:S(2)}) async-start(s8[5308416]{0:T(1024)(128)(4,1)} %bitcast.64), calls=%async_computation | async-start | bytes 8388608
  103.2 15.6 %slice-start.1 = ((s8[5308416]{0:T(1024)(128)(4,1)}), s8[1114112]{0:T(1024)(128)(4,1)S(1)}, s32[]{:S(2)}) async-start(s8[5308416]{0:T(1024)(128)(4,1)} %bitcast.64), calls=%async_computation.1 | async-start | bytes 2228224
  118.8 1.6 copy-start.5
  118.8 1.6 copy-start.9
  118.8 1.6 copy-start.10
  118.9 1.6 copy-start.16
  118.9 1.6 copy-start.19
  118.9 1.6 copy-start.21
  118.9 2.1 %copy-start.23 = (f32[256]{0:T(256)S(1)}, f32[256]{0:T(256)}, u32[]{:S(2)}) copy-start(f32[256]{0:T(256)} %copy-done.22) | copy-start | bytes 3076
  126.2 2.4 %copy-start.6 = (f32[8,1792]{1,0:T(8,128)S(1)}, f32[8,1792]{1,0:T(8,128)}, u32[]{:S(2)}) copy-start(f32[8,1792]{1,0:T(8,128)} %copy-done.5) | copy-start | bytes 172036
  (2 other events, 1.2 us)
